TPU v7x, 32 devices: a whole 2x2x4 slice. The times are simulated.
32 devices in a mesh: row: 8 (over y, x, core), col: 4 (over z).
Axes of the slice: x: 2, y: 2, z: 4, core: 2. Of those that a mesh axis runs over, the one named last changes fastest.
Arguments:
- eigvec: float32 [8192, 1024], P('row', 'col'), may hold values from -6 to 6
- refl: float32 [4, 8192, 256], P(None, ('row', 'col')), may hold values from -0.25 to 0.25
- tfac: float32 [4, 4096, 256], P(None, ('row', 'col')), may hold values from -0.375 to 0.375
- sched: int32 [16, 4], P('row'), may hold values from 0 to 3, each once within a row
Outputs:
- result: float32 [8192, 1024], P('row', 'col')
Inputs may be any that keep to these rules, and one draw needn't show every extreme that they name: Each row of sched names every slot 0 to 3 exactly once.
All inputs are finite; a program needn't handle non-finite values.
Results may differ from a plain program's by a relative error of at most 0.0002.
Values sent between devices are 32-bit elements; how exact they have to be, the bound alone decides.
A program may use at most 64 MiB of HBM per device.

v0:
```python
import functools

import jax
import jax.numpy as jnp
from jax import lax
from jax.experimental import pallas as pl
from jax.experimental.pallas import tpu as pltpu
from jax.sharding import PartitionSpec as P

B = 512
W = 256
MESH = pl.DeviceIdType.MESH


def split(x):
    high = x.astype(jnp.bfloat16)
    low = (x - high.astype(jnp.float32)).astype(jnp.bfloat16)
    return high, low


def product(left, right, dims):
    def one(a, b):
        return lax.dot_general(a, b, (dims, ((), ())), preferred_element_type=jnp.float32)

    return one(left[0], right[0]) + (one(left[0], right[1]) + one(left[1], right[0]))


def pick_kernel(slots, refl, tfac, packed, hold, in_sem, out_sem):
    steps = packed.shape[0]
    v_rows = refl.shape[1]
    t_rows = tfac.shape[1]
    loads, stores = [], []
    for s in range(steps):
        slot = slots[s]
        loads.append(
            (
                pltpu.make_async_copy(refl.at[slot], hold.at[s, pl.ds(0, v_rows)], in_sem.at[s, 0]),
                pltpu.make_async_copy(tfac.at[slot], hold.at[s, pl.ds(v_rows, t_rows)], in_sem.at[s, 1]),
            )
        )
        stores.append(pltpu.make_async_copy(hold.at[s], packed.at[s], out_sem.at[s]))
    for pair in loads:
        for copy in pair:
            copy.start()
    for pair, store in zip(loads, stores):
        for copy in pair:
            copy.wait()
        store.start()
    for store in stores:
        store.wait()


def main_kernel(n, rows_n, groups, packed, eig, out, field, buf, inb, back, landed, own_sem, eig_sem, out_sem,
                ring_send, ring_recv, up_send, up_recv, down_send, down_recv):
    steps, piece, _ = packed.shape
    v_rows = groups * B // n
    per_group = n // groups
    half = piece // 2
    hops = n // 2
    row = lax.axis_index("row")
    col = lax.axis_index("col")
    right = lax.rem(col + 1, n)
    left = lax.rem(col + n - 1, n)
    has_down = row < rows_n - 1
    has_up = row > 0
    down = jnp.minimum(row + 1, rows_n - 1)
    up = jnp.maximum(row - 1, 0)

    eig_copy = pltpu.make_async_copy(eig, field, eig_sem)
    eig_copy.start()

    barrier = pltpu.get_barrier_semaphore()
    pl.semaphore_signal(barrier, inc=1, device_id=(row, left), device_id_type=MESH)
    pl.semaphore_signal(barrier, inc=1, device_id=(row, right), device_id_type=MESH)

    @pl.when(has_up)
    def _():
        pl.semaphore_signal(barrier, inc=1, device_id=(up, col), device_id_type=MESH)

    @pl.when(has_down)
    def _():
        pl.semaphore_signal(barrier, inc=1, device_id=(down, col), device_id_type=MESH)

    pl.semaphore_wait(barrier, 2 + jnp.minimum(row, 1) + jnp.minimum(rows_n - 1 - row, 1))

    def ring_copy(s, way, hop, part):
        target = right if way == 0 else left
        owner = lax.rem(col + n - hop, n) if way == 0 else lax.rem(col + hop, n)
        span = pl.ds(part * half, half)
        src = packed.at[s, span] if hop == 0 else buf.at[s, owner, span]
        return pltpu.make_async_remote_copy(
            src_ref=src,
            dst_ref=buf.at[s, owner, span],
            send_sem=ring_send.at[s, way, hop, part],
            recv_sem=ring_recv.at[s, way, hop, part],
            device_id=(row, target),
            device_id_type=MESH,
        )

    def parts_of(way, hop):
        order = (0, 1) if way == 0 else (1, 0)
        return order[:1] if hop == hops - 1 else order

    def send_own(s):
        for k in range(len(parts_of(0, 0))):
            for way in (0, 1):
                ring_copy(s, way, 0, parts_of(way, 0)[k]).start()

    def forward(s):
        for hop in range(1, hops):
            for k in range(len(parts_of(0, hop))):
                for way in (0, 1):
                    part = parts_of(way, hop)[k]
                    ring_copy(s, way, hop - 1, part).wait_recv()
                    ring_copy(s, way, hop, part).start()

    def finish(s):
        for hop in range(hops):
            for way in (0, 1):
                done = parts_of(way, hop + 1) if hop + 1 < hops else ()
                for part in parts_of(way, hop):
                    if part not in done:
                        ring_copy(s, way, hop, part).wait_recv()

    def vectors_of(s, g):
        block = buf[s, g * per_group:(g + 1) * per_group, :v_rows]
        return split(block.reshape(B, W))

    def factor_of(s, g):
        block = buf[s, g * per_group:(g + 1) * per_group, v_rows:]
        return split(block.reshape(W, W))

    def coeffs_of(s, g, vectors, rows):
        coupling = product(vectors, split(rows), ((0,), (0,)))
        return split(product(factor_of(s, g), split(coupling), ((1,), (0,))))

    def apply_local(s, g, start):
        vectors = vectors_of(s, g)
        rows = field[start:start + B]
        coeffs = coeffs_of(s, g, vectors, rows)
        field[start:start + B] = rows - product(vectors, coeffs, ((1,), (0,)))

    def up_copy(i):
        return pltpu.make_async_remote_copy(
            src_ref=field.at[pl.ds(0, W)], dst_ref=inb.at[i],
            send_sem=up_send.at[i], recv_sem=up_recv.at[i],
            device_id=(up, col), device_id_type=MESH,
        )

    def down_copy(i):
        return pltpu.make_async_remote_copy(
            src_ref=back.at[i], dst_ref=landed.at[i],
            send_sem=down_send.at[i], recv_sem=down_recv.at[i],
            device_id=(down, col), device_id_type=MESH,
        )

    low = groups * B - W

    send_own(0)
    own = [pltpu.make_async_copy(packed.at[s], buf.at[s, col], own_sem.at[s]) for s in range(steps)]
    for copy in own:
        copy.start()
    eig_copy.wait()
    for s in range(steps):
        forward(s)
        if s + 1 < steps:
            send_own(s + 1)
        own[s].wait()
        finish(s)
        i = s // 2
        if s % 2 == 0:
            for g in range(groups):
                apply_local(s, g, g * B)
                if g == 0 and s + 1 < steps:
                    @pl.when(has_up)
                    def _():
                        up_copy(i).start()
        else:
            @pl.when(has_down)
            def _():
                up_copy(i).wait_recv()
                g = groups - 1
                vectors = vectors_of(s, g)
                rows = jnp.concatenate([field[low:], inb[i]], axis=0)
                coeffs = coeffs_of(s, g, vectors, rows)
                bottom = (vectors[0][W:], vectors[1][W:])
                back[i] = rows[W:] - product(bottom, coeffs, ((1,), (0,)))
                down_copy(i).start()
                top = (vectors[0][:W], vectors[1][:W])
                field[low:] = rows[:W] - product(top, coeffs, ((1,), (0,)))

            for g in range(groups - 1):
                apply_local(s, g, W + g * B)

            @pl.when(has_up)
            def _():
                up_copy(i).wait_send()
                down_copy(i).wait_recv()
                field[:W] = landed[i]

    store = pltpu.make_async_copy(field, out, out_sem)
    store.start()
    for s in range(steps):
        for way in (0, 1):
            for hop in range(hops):
                for part in parts_of(way, hop):
                    ring_copy(s, way, hop, part).wait_send()

    @pl.when(has_down)
    def _():
        for i in range(steps // 2):
            down_copy(i).wait_send()

    store.wait()


def line_kernel(rows_n, packed, eig, out, field, buf, inb, back, landed, own_sem, eig_sem, out_sem,
                feed_send, feed_recv, cols_send, cols_recv, cross_send, cross_recv,
                up_send, up_recv, down_send, down_recv, res_send, res_recv):
    steps, piece, _ = packed.shape
    v_rows = B // 2
    low = B + W
    last = steps - 1
    row = lax.axis_index("row")
    col = lax.axis_index("col")
    inner = (col == 1) | (col == 2)
    partner = col + 1 - 2 * lax.rem(col, 2)
    other = 3 - col
    has_down = row < rows_n - 1
    has_up = row > 0
    down = jnp.minimum(row + 1, rows_n - 1)
    up = jnp.maximum(row - 1, 0)

    def remote(src, dst, send, recv, target):
        return pltpu.make_async_remote_copy(
            src_ref=src, dst_ref=dst, send_sem=send, recv_sem=recv,
            device_id=target, device_id_type=MESH,
        )

    def greet(target):
        pl.semaphore_signal(barrier, inc=1, device_id=target, device_id_type=MESH)

    barrier = pltpu.get_barrier_semaphore()
    some_up = jnp.minimum(row, 1)
    some_down = jnp.minimum(rows_n - 1 - row, 1)
    greet((row, partner))

    @pl.when(inner)
    def _():
        greet((row, other))

        @pl.when(has_up)
        def _():
            greet((up, col))

        @pl.when(has_down)
        def _():
            greet((down, col))
            greet((down, partner))

    @pl.when(jnp.logical_not(inner) & has_up)
    def _():
        greet((up, partner))

    @pl.when(inner)
    def _():
        pl.semaphore_wait(barrier, 2 + some_up + 2 * some_down)

    @pl.when(jnp.logical_not(inner))
    def _():
        pl.semaphore_wait(barrier, 1 + some_up)

    def feed(s, owner):
        return remote(packed.at[s], buf.at[s, owner], feed_send.at[s], feed_recv.at[s], (row, partner))

    def columns(g):
        span = pl.ds(g * B, B)
        return remote(eig.at[span], field.at[1, span], cols_send.at[g], cols_recv.at[g], (row, partner))

    def cross(s, k):
        owner = col if k == 0 else partner
        src = packed.at[s] if k == 0 else buf.at[s, owner]
        return remote(src, buf.at[s, owner], cross_send.at[s, k], cross_recv.at[s, k], (row, other))

    def result(part, src, target_row):
        span = (pl.ds(0, W), pl.ds(W, B), pl.ds(low, W))[part]
        return remote(src, out.at[span], res_send.at[part], res_recv.at[part], (target_row, partner))

    @pl.when(jnp.logical_not(inner))
    def _():
        feed(0, col).start()
        columns(0).start()
        feed(1, col).start()
        feed(2, col).start()
        columns(1).start()
        feed(3, col).start()
        for s in range(steps):
            feed(s, col).wait_send()
        columns(0).wait_send()
        columns(1).wait_send()
        for part in range(3):
            rows = (W, B, W)[part]
            result(part, field.at[0, pl.ds(0, rows)], row).wait_recv()

    def vectors_of(s, g):
        return split(buf[s, 2 * g:2 * g + 2, :v_rows].reshape(B, W))

    def factor_of(s, g):
        return split(buf[s, 2 * g:2 * g + 2, v_rows:].reshape(W, W))

    def coeffs_of(vectors, factor, rows):
        coupling = product(vectors, split(rows), ((0,), (0,)))
        return split(product(factor, split(coupling), ((1,), (0,))))

    def apply_local(s, g, z, start):
        vectors = vectors_of(s, g)
        rows = field[z, start:start + B]
        coeffs = coeffs_of(vectors, factor_of(s, g), rows)
        field[z, start:start + B] = rows - product(vectors, coeffs, ((1,), (0,)))

    def up_copy(i, z):
        return remote(field.at[z, pl.ds(0, W)], inb.at[i, z], up_send.at[i, z], up_recv.at[i, z], (up, col))

    def down_copy(i, z):
        return remote(back.at[i, z], landed.at[i, z], down_send.at[i, z], down_recv.at[i, z], (down, col))

    def even(s, z):
        for g in range(2):
            apply_local(s, g, z, g * B)
            if g == 0:
                @pl.when(has_up)
                def _():
                    up_copy(s // 2, z).start()

    def straddle(s, z, send):
        i = s // 2

        @pl.when(has_down)
        def _():
            up_copy(i, z).wait_recv()
            vectors = vectors_of(s, 1)
            rows = jnp.concatenate([field[z, low:], inb[i, z]], axis=0)
            coeffs = coeffs_of(vectors, factor_of(s, 1), rows)
            bottom = (vectors[0][W:], vectors[1][W:])
            back[i, z] = rows[W:] - product(bottom, coeffs, ((1,), (0,)))
            send()
            top = (vectors[0][:W], vectors[1][:W])
            field[z, low:] = rows[:W] - product(top, coeffs, ((1,), (0,)))

    def settle(s, z):
        @pl.when(has_up)
        def _():
            up_copy(s // 2, z).wait_send()
            down_copy(s // 2, z).wait_recv()
            field[z, :W] = landed[s // 2, z]

    @pl.when(inner)
    def _():
        eig_copy = pltpu.make_async_copy(eig, field.at[0], eig_sem)
        own = [pltpu.make_async_copy(packed.at[s], buf.at[s, col], own_sem.at[s]) for s in range(steps)]

        def near(s):
            own[s].wait()

        def far(s):
            for k in range(2):
                cross(s, k).wait_recv()

        def relay(s):
            feed(s, partner).wait_recv()
            cross(s, 1).start()

        cross(0, 0).start()
        eig_copy.start()
        for copy in own:
            copy.start()
        cross(1, 0).start()
        relay(0)
        cross(2, 0).start()
        eig_copy.wait()
        near(0)
        far(0)
        even(0, 0)
        columns(0).wait_recv()
        apply_local(0, 0, 1, 0)

        @pl.when(has_up)
        def _():
            up_copy(0, 1).start()

        relay(1)
        relay(2)
        cross(3, 0).start()
        near(1)
        far(1)
        straddle(1, 0, lambda: down_copy(0, 0).start())
        apply_local(1, 0, 0, W)
        columns(1).wait_recv()
        apply_local(0, 1, 1, B)
        straddle(1, 1, lambda: down_copy(0, 1).start())
        apply_local(1, 0, 1, W)
        settle(1, 0)
        settle(1, 1)

        @pl.when(lax.rem(row, 2) == 0)
        def _():
            relay(3)

        near(2)
        far(2)
        even(2, 1)

        @pl.when(lax.rem(row, 2) == 1)
        def _():
            relay(3)

        even(2, 0)
        near(3)

        def last_straddle():
            i = last // 2
            straddle(last, 1, lambda: result(0, back.at[i, 1], down).start())
            result(2, field.at[1, pl.ds(low, W)], row).start()
            straddle(last, 0, lambda: down_copy(i, 0).start())

            @pl.when(has_up)
            def _():
                up_copy(i, 1).wait_send()
                up_copy(i, 0).wait_send()

            @pl.when(jnp.logical_not(has_up))
            def _():
                result(0, field.at[1, pl.ds(0, W)], row).start()

        def last_local():
            apply_local(last, 0, 1, W)
            result(1, field.at[1, pl.ds(W, B)], row).start()
            apply_local(last, 0, 0, W)

        @pl.when(col == 1)
        def _():
            last_local()
            far(last)
            last_straddle()

        @pl.when(col == 2)
        def _():
            last_straddle()
            far(last)
            last_local()

        @pl.when(has_up)
        def _():
            down_copy(last // 2, 0).wait_recv()
            field[0, :W] = landed[last // 2, 0]

        store = pltpu.make_async_copy(field.at[0], out, out_sem)
        store.start()
        for s in range(steps):
            for k in range(2):
                cross(s, k).wait_send()

        @pl.when(has_down)
        def _():
            down_copy(0, 0).wait_send()
            down_copy(0, 1).wait_send()
            down_copy(last // 2, 0).wait_send()
            result(0, back.at[last // 2, 1], down).wait_send()

        @pl.when(jnp.logical_not(has_up))
        def _():
            result(0, field.at[1, pl.ds(0, W)], row).wait_send()

        result(1, field.at[1, pl.ds(W, B)], row).wait_send()
        result(2, field.at[1, pl.ds(low, W)], row).wait_send()
        store.wait()


def on_device(n, rows_n, eigvec, refl, tfac, sched):
    steps, v_rows, _ = refl.shape
    t_rows = tfac.shape[1]
    groups = sched.shape[0]
    evcount = eigvec.shape[1]
    piece = v_rows + t_rows
    hops = n // 2
    owner = lax.axis_index("col") * v_rows // B
    slots = lax.dynamic_index_in_dim(sched, owner, 0, keepdims=False)
    anywhere = pl.BlockSpec(memory_space=pl.ANY)
    packed = pl.pallas_call(
        pick_kernel,
        out_shape=jax.ShapeDtypeStruct((steps, piece, W), jnp.float32),
        in_specs=[pl.BlockSpec(memory_space=pltpu.SMEM), anywhere, anywhere],
        out_specs=anywhere,
        scratch_shapes=[
            pltpu.VMEM((steps, piece, W), jnp.float32),
            pltpu.SemaphoreType.DMA((steps, 2)),
            pltpu.SemaphoreType.DMA((steps,)),
        ],
        name="pick",
    )(slots, refl, tfac)
    half_steps = steps // 2
    if n == 4 and groups == 2 and steps == 4:
        two = (half_steps, 2)
        return pl.pallas_call(
            functools.partial(line_kernel, rows_n),
            out_shape=jax.ShapeDtypeStruct(eigvec.shape, jnp.float32),
            in_specs=[anywhere, anywhere],
            out_specs=anywhere,
            scratch_shapes=[
                pltpu.VMEM((2, *eigvec.shape), jnp.float32),
                pltpu.VMEM((steps, n, piece, W), jnp.float32),
                pltpu.VMEM((*two, W, evcount), jnp.float32),
                pltpu.VMEM((*two, W, evcount), jnp.float32),
                pltpu.VMEM((*two, W, evcount), jnp.float32),
                pltpu.SemaphoreType.DMA((steps,)),
                pltpu.SemaphoreType.DMA,
                pltpu.SemaphoreType.DMA,
                pltpu.SemaphoreType.DMA((steps,)),
                pltpu.SemaphoreType.DMA((steps,)),
                pltpu.SemaphoreType.DMA((2,)),
                pltpu.SemaphoreType.DMA((2,)),
                pltpu.SemaphoreType.DMA((steps, 2)),
                pltpu.SemaphoreType.DMA((steps, 2)),
                pltpu.SemaphoreType.DMA(two),
                pltpu.SemaphoreType.DMA(two),
                pltpu.SemaphoreType.DMA(two),
                pltpu.SemaphoreType.DMA(two),
                pltpu.SemaphoreType.DMA((3,)),
                pltpu.SemaphoreType.DMA((3,)),
            ],
            compiler_params=pltpu.CompilerParams(
                collective_id=0, has_side_effects=True, vmem_limit_bytes=48 << 20
            ),
            name="sweep",
        )(packed, eigvec)
    return pl.pallas_call(
        functools.partial(main_kernel, n, rows_n, groups),
        out_shape=jax.ShapeDtypeStruct(eigvec.shape, jnp.float32),
        in_specs=[anywhere, anywhere],
        out_specs=anywhere,
        scratch_shapes=[
            pltpu.VMEM(eigvec.shape, jnp.float32),
            pltpu.VMEM((steps, n, piece, W), jnp.float32),
            pltpu.VMEM((half_steps, W, evcount), jnp.float32),
            pltpu.VMEM((half_steps, W, evcount), jnp.float32),
            pltpu.VMEM((half_steps, W, evcount), jnp.float32),
            pltpu.SemaphoreType.DMA((steps,)),
            pltpu.SemaphoreType.DMA,
            pltpu.SemaphoreType.DMA,
            pltpu.SemaphoreType.DMA((steps, 2, hops, 2)),
            pltpu.SemaphoreType.DMA((steps, 2, hops, 2)),
            pltpu.SemaphoreType.DMA((half_steps,)),
            pltpu.SemaphoreType.DMA((half_steps,)),
            pltpu.SemaphoreType.DMA((half_steps,)),
            pltpu.SemaphoreType.DMA((half_steps,)),
        ],
        compiler_params=pltpu.CompilerParams(
            collective_id=0, has_side_effects=True, vmem_limit_bytes=48 << 20
        ),
        name="sweep",
    )(packed, eigvec)


def solution(mesh):
    placed = (
        P("row", "col"),
        P(None, ("row", "col"), None),
        P(None, ("row", "col"), None),
        P("row", None),
    )
    body = functools.partial(on_device, mesh.shape["col"], mesh.shape["row"])
    return jax.shard_map(body, mesh=mesh, in_specs=placed, out_specs=P("row", "col"), check_vma=False)
```

profile of v0, /device:TPU:24, one launch (start us, length us, event | category | flops | bytes accessed | tf_op | source)
XLA Modules:
  0.0 100.7 jit_solution(13317969851282741557)
XLA Ops:
  0.0 0.0 copy-start
  0.0 0.7 copy-done
  0.7 0.5 dynamic-slice_bitcast_fusion.slots
  1.2 0.0 copy-start.2
  1.2 3.1 %pick.1.packed = f32[4,384,256]{2,1,0:T(8,128)} custom-call(s32[4]{0:T(128)} %dynamic-slice_bitcast_fusion.slots, f32[4,256,256]{2,1,0:T(8,128)} %refl.1, f32[4,128,256]{2,1,0:T(8,128)} %tfac.1), custom_call_target="tpu_custom_call" | custom-call | tf_op jit(solution)/shard_map/pick/pallas_call | solution.py:489
  4.3 0.0 copy-done.2
  4.3 0.0 copy-start.1
  4.3 1.4 %copy-done.1 = f32[4,384,256]{2,1,0:T(8,128)S(1)} copy-done((f32[4,384,256]{2,1,0:T(8,128)S(1)}, f32[4,384,256]{2,1,0:T(8,128)}, u32[]{:S(2)}) %copy-start.1) | copy-done | bytes 1572888
  5.7 94.0 %sweep.1 = f32[1024,256]{1,0:T(8,128)S(1)} custom-call(f32[4,384,256]{2,1,0:T(8,128)S(1)} %copy-done.1, f32[1024,256]{1,0:T(8,128)S(1)} %copy-done.2), custom_call_target="tpu_custom_call" | custom-call | tf_op jit(solution)/shard_map/sweep/pallas_call | solution.py:504
  99.7 1.0 copy.6
Async XLA Ops:
  0.0 0.7 copy-start
  1.2 3.1 %copy-start.2 = (f32[1024,256]{1,0:T(8,128)S(1)}, f32[1024,256]{1,0:T(8,128)}, u32[]{:S(2)}) copy-start(f32[1024,256]{1,0:T(8,128)} %eig.1) | copy-start | bytes 3145732
  4.3 1.4 %copy-start.1 = (f32[4,384,256]{2,1,0:T(8,128)S(1)}, f32[4,384,256]{2,1,0:T(8,128)}, u32[]{:S(2)}) copy-start(f32[4,384,256]{2,1,0:T(8,128)} %pick.1.packed) | copy-start | bytes 4718596
where the time goes:
time: 101 us
  Pallas kernels  97.1 us (96%)
  local copies, waits for them, and re-layouts  3.57 us (4%)
    pallas_call x1, Pallas kernels, on_device(): pl.pallas_call(functools.partial(line_kernel, rows_n), out_shape=jax.Shap...  94 us
    pallas_call x1, Pallas kernels, on_device(): pl.pallas_call(pick_kernel, out_shape=jax.ShapeDtypeStruct((steps, piece,...  3.08 us
    unnamed x7, local copies, waits for them, and re-layouts  3.06 us

commit v1 on v0

--- a/solution.py
+++ b/solution.py
@@ -214,18 +214,24 @@
     store.wait()
 
 
-def line_kernel(rows_n, packed, eig, out, field, buf, inb, back, landed, own_sem, eig_sem, out_sem,
-                feed_send, feed_recv, cols_send, cols_recv, cross_send, cross_recv,
-                up_send, up_recv, down_send, down_recv, res_send, res_recv):
-    steps, piece, _ = packed.shape
-    v_rows = B // 2
+def line_kernel(rows_n, sched, refl, tfac, eig, out, refl_in, tfac_in, field, buf, fed, inb, back, landed,
+                load_sem, eig_sem, out_sem, feed_send, feed_recv, cols_send, cols_recv, own_send, own_recv,
+                relay_send, relay_recv, hand_send, hand_recv, up_send, up_recv, down_send, down_recv,
+                res_send, res_recv, share_send, share_recv, state_send, state_recv):
+    steps, v_rows, _ = refl.shape
     low = B + W
     last = steps - 1
     row = lax.axis_index("row")
     col = lax.axis_index("col")
+    odd = lax.rem(row, 2)
     inner = (col == 1) | (col == 2)
     partner = col + 1 - 2 * lax.rem(col, 2)
     other = 3 - col
+    mate = row + 1 - 2 * odd
+    beyond = row - 1 + 2 * odd
+    has_beyond = (beyond >= 0) & (beyond < rows_n)
+    beyond = jnp.clip(beyond, 0, rows_n - 1)
+    own_first = (col == 1) == (odd == 0)
     has_down = row < rows_n - 1
     has_up = row > 0
     down = jnp.minimum(row + 1, rows_n - 1)
@@ -237,70 +243,78 @@
             device_id=target, device_id_type=MESH,
         )
 
+    refl_load = pltpu.make_async_copy(refl, refl_in, load_sem.at[0])
+    tfac_load = pltpu.make_async_copy(tfac, tfac_in, load_sem.at[1])
+    eig_load = pltpu.make_async_copy(eig, field.at[0], eig_sem)
+    refl_load.start()
+    tfac_load.start()
+
+    barrier = pltpu.get_barrier_semaphore()
+
     def greet(target):
         pl.semaphore_signal(barrier, inc=1, device_id=target, device_id_type=MESH)
 
-    barrier = pltpu.get_barrier_semaphore()
-    some_up = jnp.minimum(row, 1)
-    some_down = jnp.minimum(rows_n - 1 - row, 1)
     greet((row, partner))
+    greet((mate, partner))
+    greet((mate, col))
+
+    @pl.when(has_beyond)
+    def _():
+        greet((beyond, col))
+        greet((beyond, partner))
 
     @pl.when(inner)
     def _():
         greet((row, other))
-
-        @pl.when(has_up)
-        def _():
-            greet((up, col))
-
-        @pl.when(has_down)
-        def _():
-            greet((down, col))
-            greet((down, partner))
-
-    @pl.when(jnp.logical_not(inner) & has_up)
-    def _():
-        greet((up, partner))
-
-    @pl.when(inner)
-    def _():
-        pl.semaphore_wait(barrier, 2 + some_up + 2 * some_down)
-
-    @pl.when(jnp.logical_not(inner))
-    def _():
-        pl.semaphore_wait(barrier, 1 + some_up)
-
-    def feed(s, owner):
-        return remote(packed.at[s], buf.at[s, owner], feed_send.at[s], feed_recv.at[s], (row, partner))
+        greet((mate, other))
+        eig_load.start()
+
+    refl_load.wait()
+    tfac_load.wait()
+    for s in range(steps):
+        slot = sched[col // 2, s]
+        buf[s, col, :v_rows] = refl_in[slot]
+        buf[s, col, v_rows:] = tfac_in[slot]
+
+    pl.semaphore_wait(barrier, 3 + 2 * has_beyond.astype(jnp.int32) + 2 * inner.astype(jnp.int32))
+
+    cuts = (3, 1, 1, 3)
+    piece = buf.shape[2]
+
+    def span(s, k):
+        size = piece // cuts[s]
+        return pl.ds(k * size, size)
+
+    def feed(s, k):
+        return remote(buf.at[s, col, span(s, k)], fed.at[s, span(s, k)],
+                      feed_send.at[s, k], feed_recv.at[s, k], (mate, partner))
 
     def columns(g):
-        span = pl.ds(g * B, B)
-        return remote(eig.at[span], field.at[1, span], cols_send.at[g], cols_recv.at[g], (row, partner))
-
-    def cross(s, k):
-        owner = col if k == 0 else partner
-        src = packed.at[s] if k == 0 else buf.at[s, owner]
-        return remote(src, buf.at[s, owner], cross_send.at[s, k], cross_recv.at[s, k], (row, other))
+        rows = pl.ds(g * B, B)
+        return remote(eig.at[rows], field.at[1, rows], cols_send.at[g], cols_recv.at[g], (row, partner))
+
+    def own(s):
+        return remote(buf.at[s, col], buf.at[s, col], own_send.at[s], own_recv.at[s], (row, other))
+
+    def own_arrival(s):
+        return remote(buf.at[s, other], buf.at[s, other], own_send.at[s], own_recv.at[s], (row, other))
+
+    def relay(s, k):
+        return remote(fed.at[s, span(s, k)], buf.at[s, partner, span(s, k)],
+                      relay_send.at[s, k], relay_recv.at[s, k], (mate, other))
+
+    def relay_arrival(s, k):
+        owner = 3 - partner
+        return remote(fed.at[s, span(s, k)], buf.at[s, owner, span(s, k)],
+                      relay_send.at[s, k], relay_recv.at[s, k], (mate, other))
+
+    def hand(s, k):
+        return remote(fed.at[s, span(s, k)], buf.at[s, partner, span(s, k)],
+                      hand_send.at[s, k], hand_recv.at[s, k], (mate, col))
 
     def result(part, src, target_row):
-        span = (pl.ds(0, W), pl.ds(W, B), pl.ds(low, W))[part]
-        return remote(src, out.at[span], res_send.at[part], res_recv.at[part], (target_row, partner))
-
-    @pl.when(jnp.logical_not(inner))
-    def _():
-        feed(0, col).start()
-        columns(0).start()
-        feed(1, col).start()
-        feed(2, col).start()
-        columns(1).start()
-        feed(3, col).start()
-        for s in range(steps):
-            feed(s, col).wait_send()
-        columns(0).wait_send()
-        columns(1).wait_send()
-        for part in range(3):
-            rows = (W, B, W)[part]
-            result(part, field.at[0, pl.ds(0, rows)], row).wait_recv()
+        rows = (pl.ds(0, W), pl.ds(W, B), pl.ds(low, W))[part]
+        return remote(src, out.at[rows], res_send.at[part], res_recv.at[part], (target_row, partner))
 
     def vectors_of(s, g):
         return split(buf[s, 2 * g:2 * g + 2, :v_rows].reshape(B, W))
@@ -312,168 +326,349 @@
         coupling = product(vectors, split(rows), ((0,), (0,)))
         return split(product(factor, split(coupling), ((1,), (0,))))
 
-    def apply_local(s, g, z, start):
+    def load(zs, start, size):
+        return jnp.concatenate([field[z, start:start + size] for z in zs], axis=1)
+
+    def save(zs, start, value):
+        cols = value.shape[1] // len(zs)
+        for k, z in enumerate(zs):
+            field[z, start:start + value.shape[0]] = value[:, k * cols:(k + 1) * cols]
+
+    def apply_local(s, g, zs, start):
         vectors = vectors_of(s, g)
-        rows = field[z, start:start + B]
+        rows = load(zs, start, B)
         coeffs = coeffs_of(vectors, factor_of(s, g), rows)
-        field[z, start:start + B] = rows - product(vectors, coeffs, ((1,), (0,)))
+        save(zs, start, rows - product(vectors, coeffs, ((1,), (0,))))
 
     def up_copy(i, z):
         return remote(field.at[z, pl.ds(0, W)], inb.at[i, z], up_send.at[i, z], up_recv.at[i, z], (up, col))
 
-    def down_copy(i, z):
-        return remote(back.at[i, z], landed.at[i, z], down_send.at[i, z], down_recv.at[i, z], (down, col))
-
-    def even(s, z):
-        for g in range(2):
-            apply_local(s, g, z, g * B)
-            if g == 0:
-                @pl.when(has_up)
-                def _():
-                    up_copy(s // 2, z).start()
-
-    def straddle(s, z, send):
+    def down_copy(z):
+        return remote(back.at[0, z], landed.at[z], down_send.at[0, z], down_recv.at[0, z], (down, col))
+
+    def down_final():
+        return remote(back.at[1, 0], out.at[pl.ds(0, W)], down_send.at[1, 0], down_recv.at[1, 0], (down, col))
+
+    def send_up(s, zs):
+        @pl.when(has_up)
+        def _():
+            for z in zs:
+                up_copy(s // 2, z).start()
+
+    def straddle_body(s, zs, send):
         i = s // 2
-
+        vectors = vectors_of(s, 1)
+        below = jnp.concatenate([inb[i, z] for z in zs], axis=1)
+        rows = jnp.concatenate([load(zs, low, W), below], axis=0)
+        coeffs = coeffs_of(vectors, factor_of(s, 1), rows)
+        bottom = (vectors[0][W:], vectors[1][W:])
+        value = rows[W:] - product(bottom, coeffs, ((1,), (0,)))
+        cols = value.shape[1] // len(zs)
+        for k, z in enumerate(zs):
+            back[i, z] = value[:, k * cols:(k + 1) * cols]
+        send()
+        top = (vectors[0][:W], vectors[1][:W])
+        save(zs, low, rows[:W] - product(top, coeffs, ((1,), (0,))))
+
+    def straddle(s, zs, send):
         @pl.when(has_down)
         def _():
-            up_copy(i, z).wait_recv()
-            vectors = vectors_of(s, 1)
-            rows = jnp.concatenate([field[z, low:], inb[i, z]], axis=0)
-            coeffs = coeffs_of(vectors, factor_of(s, 1), rows)
-            bottom = (vectors[0][W:], vectors[1][W:])
-            back[i, z] = rows[W:] - product(bottom, coeffs, ((1,), (0,)))
-            send()
-            top = (vectors[0][:W], vectors[1][:W])
-            field[z, low:] = rows[:W] - product(top, coeffs, ((1,), (0,)))
-
-    def settle(s, z):
+            for z in zs:
+                up_copy(s // 2, z).wait_recv()
+            straddle_body(s, zs, send)
+
+    def settle(z):
         @pl.when(has_up)
         def _():
-            up_copy(s // 2, z).wait_send()
-            down_copy(s // 2, z).wait_recv()
-            field[z, :W] = landed[s // 2, z]
+            up_copy(0, z).wait_send()
+            down_copy(z).wait_recv()
+            field[z, :W] = landed[z]
+
+    def pass_chunk(s, k):
+        feed(s, k).wait_recv()
+        relay(s, k).start()
+        hand(s, k).start()
+
+    def passed(s):
+        for k in range(cuts[s]):
+            pass_chunk(s, k)
+
+    def own_before(s):
+        @pl.when(own_first)
+        def _():
+            own(s).start()
+
+    def own_after(s):
+        @pl.when(jnp.logical_not(own_first))
+        def _():
+            own(s).start()
+
+    def near(s):
+        for k in range(cuts[s]):
+            hand(s, k).wait_recv()
+
+    def far(s):
+        own_arrival(s).wait_recv()
+        for k in range(cuts[s]):
+            relay_arrival(s, k).wait_recv()
+
+    def store(part):
+        rows = (pl.ds(0, W), pl.ds(W, B), pl.ds(low, W))[part]
+        return pltpu.make_async_copy(field.at[0, rows], out.at[rows], out_sem.at[part])
+
+    def share():
+        return remote(buf.at[last, col], buf.at[last, col], share_send, share_recv, (row, partner))
+
+    def share_arrival():
+        return remote(buf.at[last, partner], buf.at[last, partner], share_send, share_recv, (row, partner))
+
+    def state(part, start):
+        rows = pl.ds(start, W)
+        return remote(field.at[1, rows], field.at[0, rows], state_send.at[part], state_recv.at[part], (row, partner))
+
+    def state_up():
+        return remote(field.at[1, pl.ds(0, W)], inb.at[1, 0], state_send.at[1], state_recv.at[1], (up, partner))
+
+    def bottom_result():
+        return remote(back.at[1, 0], out.at[pl.ds(0, W)], res_send.at[0], res_recv.at[0], (down, col))
+
+    @pl.when(jnp.logical_not(inner))
+    def _():
+        for kind, k in (("feed", 0), ("feed", 1), ("feed", 2), ("cols", 0), ("cols", 1), ("feed", 3)):
+            if kind == "feed":
+                for c in range(cuts[k]):
+                    feed(k, c).start()
+            else:
+                columns(k).start()
+        share_arrival().wait_recv()
+        state(0, W).wait_recv()
+
+        @pl.when(col == 0)
+        def _():
+            state(1, W).wait_recv()
+            apply_local(last, 0, (0,), W)
+            store(1).start()
+            result(0, field.at[0, pl.ds(0, W)], row).wait_recv()
+            result(2, field.at[0, pl.ds(0, W)], row).wait_recv()
+            store(1).wait()
+
+        @pl.when(col == 3)
+        def _():
+            @pl.when(has_down)
+            def _():
+                state_up().wait_recv()
+                straddle_body(last, (0,), lambda: bottom_result().start())
+
+            store(2).start()
+            result(0, field.at[0, pl.ds(0, W)], row).wait_recv()
+            result(1, field.at[0, pl.ds(0, B)], row).wait_recv()
+            store(2).wait()
+
+            @pl.when(has_down)
+            def _():
+                bottom_result().wait_send()
+
+        for s in range(steps):
+            for k in range(cuts[s]):
+                feed(s, k).wait_send()
+        columns(0).wait_send()
+        columns(1).wait_send()
+
+    early = jnp.logical_not(own_first)
 
     @pl.when(inner)
     def _():
-        eig_copy = pltpu.make_async_copy(eig, field.at[0], eig_sem)
-        own = [pltpu.make_async_copy(packed.at[s], buf.at[s, col], own_sem.at[s]) for s in range(steps)]
-
-        def near(s):
-            own[s].wait()
-
-        def far(s):
-            for k in range(2):
-                cross(s, k).wait_recv()
-
-        def relay(s):
-            feed(s, partner).wait_recv()
-            cross(s, 1).start()
-
-        cross(0, 0).start()
-        eig_copy.start()
-        for copy in own:
-            copy.start()
-        cross(1, 0).start()
-        relay(0)
-        cross(2, 0).start()
-        eig_copy.wait()
+        own(0).start()
+        share().start()
+        passed(0)
+        own_before(1)
+        eig_load.wait()
         near(0)
+
+        @pl.when(col == 1)
+        def _():
+            apply_local(0, 0, (0,), 0)
+            send_up(0, (0,))
+
+        @pl.when(col == 2)
+        def _():
+            apply_local(0, 1, (0,), B)
+
+        passed(1)
+        own_after(1)
+        own_before(2)
         far(0)
-        even(0, 0)
+        near(1)
+
+        @pl.when(col == 1)
+        def _():
+            apply_local(0, 1, (0,), B)
+            apply_local(1, 0, (0,), W)
+
+        @pl.when(col == 2)
+        def _():
+            apply_local(0, 0, (0,), 0)
+            send_up(0, (0,))
+            straddle(1, (0,), lambda: down_copy(0).start())
+
+        passed(2)
+        own_after(2)
+        own_before(3)
+        far(1)
+
+        @pl.when(col == 1)
+        def _():
+            straddle(1, (0,), lambda: down_copy(0).start())
+
+        @pl.when(col == 2)
+        def _():
+            apply_local(1, 0, (0,), W)
+
         columns(0).wait_recv()
-        apply_local(0, 0, 1, 0)
+        apply_local(0, 0, (1,), 0)
+        send_up(0, (1,))
+        settle(0)
+        near(2)
+
+        @pl.when(col == 1)
+        def _():
+            apply_local(2, 0, (0,), 0)
+            send_up(2, (0,))
+
+        @pl.when(col == 2)
+        def _():
+            apply_local(2, 1, (0,), B)
+
+        def far_even():
+            @pl.when(col == 1)
+            def _():
+                apply_local(2, 1, (0,), B)
+
+            @pl.when(col == 2)
+            def _():
+                apply_local(2, 0, (0,), 0)
+                send_up(2, (0,))
+
+        @pl.when(early)
+        def _():
+            far(2)
+            far_even()
+
+        columns(1).wait_recv()
+        apply_local(0, 1, (1,), B)
+        straddle(1, (1,), lambda: down_copy(1).start())
+        pass_chunk(3, 0)
+        apply_local(1, 0, (1,), W)
+
+        @pl.when(col == 2)
+        def _():
+            apply_local(2, 1, (1,), B)
+            state(0, low).start()
+
+        @pl.when(own_first)
+        def _():
+            far(2)
+
+        @pl.when(col == 1)
+        def _():
+            apply_local(2, 1, (1,), B)
+            state(0, B).start()
+
+        pass_chunk(3, 1)
+        settle(1)
+        apply_local(2, 0, (1,), 0)
+
+        @pl.when(col == 1)
+        def _():
+            state(1, W).start()
+            send_up(2, (1,))
+
+        @pl.when((col == 2) & has_up)
+        def _():
+            state_up().start()
+
+        pass_chunk(3, 2)
+        own_after(3)
+
+        @pl.when(own_first)
+        def _():
+            far_even()
+
+        @pl.when(jnp.logical_not(has_up))
+        def _():
+            result(0, field.at[1, pl.ds(0, W)], row).start()
+            store(0).start()
+
+        near(3)
+
+        @pl.when(col == 1)
+        def _():
+            apply_local(last, 0, (0,), W)
+            store(1).start()
+            far(3)
+            straddle(last, (1,), lambda: result(0, back.at[1, 1], down).start())
+            result(2, field.at[1, pl.ds(low, W)], row).start()
+            straddle(last, (0,), lambda: down_final().start())
+            store(2).start()
+
+        @pl.when(col == 2)
+        def _():
+            straddle(last, (0,), lambda: down_final().start())
+            store(2).start()
+            far(3)
+            apply_local(last, 0, (1,), W)
+            result(1, field.at[1, pl.ds(W, B)], row).start()
+            apply_local(last, 0, (0,), W)
+            store(1).start()
+
+        share().wait_send()
+        state(0, W).wait_send()
+        for s in range(steps):
+            own(s).wait_send()
+            for k in range(cuts[s]):
+                relay(s, k).wait_send()
+                hand(s, k).wait_send()
 
         @pl.when(has_up)
         def _():
-            up_copy(0, 1).start()
-
-        relay(1)
-        relay(2)
-        cross(3, 0).start()
-        near(1)
-        far(1)
-        straddle(1, 0, lambda: down_copy(0, 0).start())
-        apply_local(1, 0, 0, W)
-        columns(1).wait_recv()
-        apply_local(0, 1, 1, B)
-        straddle(1, 1, lambda: down_copy(0, 1).start())
-        apply_local(1, 0, 1, W)
-        settle(1, 0)
-        settle(1, 1)
-
-        @pl.when(lax.rem(row, 2) == 0)
-        def _():
-            relay(3)
-
-        near(2)
-        far(2)
-        even(2, 1)
-
-        @pl.when(lax.rem(row, 2) == 1)
-        def _():
-            relay(3)
-
-        even(2, 0)
-        near(3)
-
-        def last_straddle():
-            i = last // 2
-            straddle(last, 1, lambda: result(0, back.at[i, 1], down).start())
-            result(2, field.at[1, pl.ds(low, W)], row).start()
-            straddle(last, 0, lambda: down_copy(i, 0).start())
+            up_copy(last // 2, 0).wait_send()
+            down_final().wait_recv()
+
+        @pl.when(has_down)
+        def _():
+            down_copy(0).wait_send()
+            down_copy(1).wait_send()
+            down_final().wait_send()
+
+        @pl.when(jnp.logical_not(has_up))
+        def _():
+            result(0, field.at[1, pl.ds(0, W)], row).wait_send()
+            store(0).wait()
+
+        @pl.when(col == 1)
+        def _():
+            state(1, W).wait_send()
 
             @pl.when(has_up)
             def _():
-                up_copy(i, 1).wait_send()
-                up_copy(i, 0).wait_send()
-
-            @pl.when(jnp.logical_not(has_up))
-            def _():
-                result(0, field.at[1, pl.ds(0, W)], row).start()
-
-        def last_local():
-            apply_local(last, 0, 1, W)
-            result(1, field.at[1, pl.ds(W, B)], row).start()
-            apply_local(last, 0, 0, W)
-
-        @pl.when(col == 1)
-        def _():
-            last_local()
-            far(last)
-            last_straddle()
+                up_copy(last // 2, 1).wait_send()
+
+            @pl.when(has_down)
+            def _():
+                result(0, back.at[1, 1], down).wait_send()
+
+            result(2, field.at[1, pl.ds(low, W)], row).wait_send()
 
         @pl.when(col == 2)
         def _():
-            last_straddle()
-            far(last)
-            last_local()
-
-        @pl.when(has_up)
-        def _():
-            down_copy(last // 2, 0).wait_recv()
-            field[0, :W] = landed[last // 2, 0]
-
-        store = pltpu.make_async_copy(field.at[0], out, out_sem)
-        store.start()
-        for s in range(steps):
-            for k in range(2):
-                cross(s, k).wait_send()
-
-        @pl.when(has_down)
-        def _():
-            down_copy(0, 0).wait_send()
-            down_copy(0, 1).wait_send()
-            down_copy(last // 2, 0).wait_send()
-            result(0, back.at[last // 2, 1], down).wait_send()
-
-        @pl.when(jnp.logical_not(has_up))
-        def _():
-            result(0, field.at[1, pl.ds(0, W)], row).wait_send()
-
-        result(1, field.at[1, pl.ds(W, B)], row).wait_send()
-        result(2, field.at[1, pl.ds(low, W)], row).wait_send()
-        store.wait()
+            @pl.when(has_up)
+            def _():
+                state_up().wait_send()
+
+            result(1, field.at[1, pl.ds(W, B)], row).wait_send()
+
+        store(1).wait()
+        store(2).wait()
 
 
 def on_device(n, rows_n, eigvec, refl, tfac, sched):
@@ -483,9 +678,57 @@
     evcount = eigvec.shape[1]
     piece = v_rows + t_rows
     hops = n // 2
+    half_steps = steps // 2
+    anywhere = pl.BlockSpec(memory_space=pl.ANY)
+    if n == 4 and groups == 2 and steps == 4 and rows_n % 2 == 0:
+        two = (half_steps, 2)
+        chunks = (steps, 3)
+        dma = pltpu.SemaphoreType.DMA
+        return pl.pallas_call(
+            functools.partial(line_kernel, rows_n),
+            out_shape=jax.ShapeDtypeStruct(eigvec.shape, jnp.float32),
+            in_specs=[pl.BlockSpec(memory_space=pltpu.SMEM), anywhere, anywhere, anywhere],
+            out_specs=anywhere,
+            scratch_shapes=[
+                pltpu.VMEM(refl.shape, jnp.float32),
+                pltpu.VMEM(tfac.shape, jnp.float32),
+                pltpu.VMEM((2, *eigvec.shape), jnp.float32),
+                pltpu.VMEM((steps, n, piece, W), jnp.float32),
+                pltpu.VMEM((steps, piece, W), jnp.float32),
+                pltpu.VMEM((*two, W, evcount), jnp.float32),
+                pltpu.VMEM((*two, W, evcount), jnp.float32),
+                pltpu.VMEM((2, W, evcount), jnp.float32),
+                dma((2,)),
+                dma,
+                dma((3,)),
+                dma(chunks),
+                dma(chunks),
+                dma((2,)),
+                dma((2,)),
+                dma((steps,)),
+                dma((steps,)),
+                dma(chunks),
+                dma(chunks),
+                dma(chunks),
+                dma(chunks),
+                dma(two),
+                dma(two),
+                dma(two),
+                dma(two),
+                dma((3,)),
+                dma((3,)),
+                dma,
+                dma,
+                dma((2,)),
+                dma((2,)),
+            ],
+            compiler_params=pltpu.CompilerParams(
+                collective_id=0, has_side_effects=True, vmem_limit_bytes=60 << 20
+            ),
+            name="sweep",
+        )(sched, refl, tfac, eigvec)
     owner = lax.axis_index("col") * v_rows // B
     slots = lax.dynamic_index_in_dim(sched, owner, 0, keepdims=False)
-    anywhere = pl.BlockSpec(memory_space=pl.ANY)
     packed = pl.pallas_call(
         pick_kernel,
         out_shape=jax.ShapeDtypeStruct((steps, piece, W), jnp.float32),
@@ -498,41 +741,6 @@
         ],
         name="pick",
     )(slots, refl, tfac)
-    half_steps = steps // 2
-    if n == 4 and groups == 2 and steps == 4:
-        two = (half_steps, 2)
-        return pl.pallas_call(
-            functools.partial(line_kernel, rows_n),
-            out_shape=jax.ShapeDtypeStruct(eigvec.shape, jnp.float32),
-            in_specs=[anywhere, anywhere],
-            out_specs=anywhere,
-            scratch_shapes=[
-                pltpu.VMEM((2, *eigvec.shape), jnp.float32),
-                pltpu.VMEM((steps, n, piece, W), jnp.float32),
-                pltpu.VMEM((*two, W, evcount), jnp.float32),
-                pltpu.VMEM((*two, W, evcount), jnp.float32),
-                pltpu.VMEM((*two, W, evcount), jnp.float32),
-                pltpu.SemaphoreType.DMA((steps,)),
-                pltpu.SemaphoreType.DMA,
-                pltpu.SemaphoreType.DMA,
-                pltpu.SemaphoreType.DMA((steps,)),
-                pltpu.SemaphoreType.DMA((steps,)),
-                pltpu.SemaphoreType.DMA((2,)),
-                pltpu.SemaphoreType.DMA((2,)),
-                pltpu.SemaphoreType.DMA((steps, 2)),
-                pltpu.SemaphoreType.DMA((steps, 2)),
-                pltpu.SemaphoreType.DMA(two),
-                pltpu.SemaphoreType.DMA(two),
-                pltpu.SemaphoreType.DMA(two),
-                pltpu.SemaphoreType.DMA(two),
-                pltpu.SemaphoreType.DMA((3,)),
-                pltpu.SemaphoreType.DMA((3,)),
-            ],
-            compiler_params=pltpu.CompilerParams(
-                collective_id=0, has_side_effects=True, vmem_limit_bytes=48 << 20
-            ),
-            name="sweep",
-        )(packed, eigvec)
     return pl.pallas_call(
         functools.partial(main_kernel, n, rows_n, groups),
         out_shape=jax.ShapeDtypeStruct(eigvec.shape, jnp.float32),

time: 101 us -> 90.7 us (0.90)
  the two profiles are of different devices: /device:TPU:24 before, /device:TPU:0 now
where the time goes in v1:
time: 90.7 us; the launch traced here: 90.5 us
  Pallas kernels  88.3 us (97%)
  local copies, waits for them, and re-layouts  2.26 us (2%)
    pallas_call x1, Pallas kernels, on_device(): pl.pallas_call(functools.partial(line_kernel, rows_n), out_shape=jax.Shap...  88.3 us
    unnamed x1, local copies, waits for them, and re-layouts  2.26 us

profile of v1, /device:TPU:0, one launch (start us, length us, event | category | flops | bytes accessed | tf_op | source)
XLA Modules:
  0.0 90.5 jit_solution(11019603907213941231)
XLA Ops:
  0.0 88.3 %sweep.1 = f32[1024,256]{1,0:T(8,128)} custom-call(s32[2,4]{1,0:T(2,128)} %sched.1, f32[4,256,256]{2,1,0:T(8,128)} %refl.1, f32[4,128,256]{2,1,0:T(8,128)} %tfac.1, f32[1024,256]{1,0:T(8,128)} %eig.1), custom_call_target="tpu_custom_call" | custom-call | tf_op jit(solution)/shard_map/sweep/pallas_call | solution.py:687
  88.3 2.3 %copy.6 = f32[1024,256]{1,0:T(8,128)} copy(f32[1024,256]{1,0:T(8,128)} %sweep.1) | data formatting | bytes 2097152

commit v2 on v1

--- a/solution.py
+++ b/solution.py
@@ -214,10 +214,10 @@
     store.wait()
 
 
-def line_kernel(rows_n, sched, refl, tfac, eig, out, refl_in, tfac_in, field, buf, fed, inb, back, landed,
+def line_kernel(rows_n, sched_all, refl, tfac, eig, out, sched, refl_in, tfac_in, field, buf, fed, inb, back, landed,
                 load_sem, eig_sem, out_sem, feed_send, feed_recv, cols_send, cols_recv, own_send, own_recv,
                 relay_send, relay_recv, hand_send, hand_recv, up_send, up_recv, down_send, down_recv,
-                res_send, res_recv, share_send, share_recv, state_send, state_recv):
+                res_send, res_recv, share_send, share_recv, state_send, state_recv, turn_sem):
     steps, v_rows, _ = refl.shape
     low = B + W
     last = steps - 1
@@ -246,6 +246,8 @@
     refl_load = pltpu.make_async_copy(refl, refl_in, load_sem.at[0])
     tfac_load = pltpu.make_async_copy(tfac, tfac_in, load_sem.at[1])
     eig_load = pltpu.make_async_copy(eig, field.at[0], eig_sem)
+    sched_load = pltpu.make_async_copy(sched_all, sched, load_sem.at[2])
+    sched_load.start()
     refl_load.start()
     tfac_load.start()
 
@@ -267,10 +269,15 @@
     def _():
         greet((row, other))
         greet((mate, other))
-        eig_load.start()
-
+
+    sched_load.wait()
     refl_load.wait()
     tfac_load.wait()
+
+    @pl.when(inner)
+    def _():
+        eig_load.start()
+
     for s in range(steps):
         slot = sched[col // 2, s]
         buf[s, col, :v_rows] = refl_in[slot]
@@ -289,15 +296,29 @@
         return remote(buf.at[s, col, span(s, k)], fed.at[s, span(s, k)],
                       feed_send.at[s, k], feed_recv.at[s, k], (mate, partner))
 
+    column_rows = ((0, B), (B, W), (B + W, W))
+
     def columns(g):
-        rows = pl.ds(g * B, B)
+        rows = pl.ds(*column_rows[g])
         return remote(eig.at[rows], field.at[1, rows], cols_send.at[g], cols_recv.at[g], (row, partner))
 
-    def own(s):
-        return remote(buf.at[s, col], buf.at[s, col], own_send.at[s], own_recv.at[s], (row, other))
-
-    def own_arrival(s):
-        return remote(buf.at[s, other], buf.at[s, other], own_send.at[s], own_recv.at[s], (row, other))
+    own_cuts = (1, 1, 1, 3)
+
+    def own_span(s, k):
+        size = piece // own_cuts[s]
+        return pl.ds(k * size, size)
+
+    def own(s, k):
+        part = buf.at[s, col, own_span(s, k)]
+        return remote(part, part, own_send.at[s, k], own_recv.at[s, k], (row, other))
+
+    def own_arrival(s, k):
+        part = buf.at[s, other, own_span(s, k)]
+        return remote(part, part, own_send.at[s, k], own_recv.at[s, k], (row, other))
+
+    def send_own(s, ks):
+        for k in ks:
+            own(s, k).start()
 
     def relay(s, k):
         return remote(fed.at[s, span(s, k)], buf.at[s, partner, span(s, k)],
@@ -393,22 +414,13 @@
         for k in range(cuts[s]):
             pass_chunk(s, k)
 
-    def own_before(s):
-        @pl.when(own_first)
-        def _():
-            own(s).start()
-
-    def own_after(s):
-        @pl.when(jnp.logical_not(own_first))
-        def _():
-            own(s).start()
-
     def near(s):
         for k in range(cuts[s]):
             hand(s, k).wait_recv()
 
     def far(s):
-        own_arrival(s).wait_recv()
+        for k in range(own_cuts[s]):
+            own_arrival(s, k).wait_recv()
         for k in range(cuts[s]):
             relay_arrival(s, k).wait_recv()
 
@@ -434,12 +446,35 @@
 
     @pl.when(jnp.logical_not(inner))
     def _():
-        for kind, k in (("feed", 0), ("feed", 1), ("feed", 2), ("cols", 0), ("cols", 1), ("feed", 3)):
-            if kind == "feed":
-                for c in range(cuts[k]):
-                    feed(k, c).start()
-            else:
-                columns(k).start()
+        def turn():
+            pl.semaphore_signal(turn_sem, inc=1, device_id=(mate, col), device_id_type=MESH)
+
+        for k in range(last):
+            for c in range(cuts[k]):
+                feed(k, c).start()
+        columns(0).start()
+
+        @pl.when(odd == 0)
+        def _():
+            pl.semaphore_wait(turn_sem, 1)
+
+        columns(1).start()
+        columns(2).start()
+        columns(1).wait_send()
+
+        @pl.when(odd == 0)
+        def _():
+            columns(2).wait_send()
+
+        turn()
+
+        @pl.when(odd == 1)
+        def _():
+            pl.semaphore_wait(turn_sem, 1)
+            columns(2).wait_send()
+
+        for c in range(cuts[last]):
+            feed(last, c).start()
         share_arrival().wait_recv()
         state(0, W).wait_recv()
 
@@ -472,16 +507,15 @@
             for k in range(cuts[s]):
                 feed(s, k).wait_send()
         columns(0).wait_send()
-        columns(1).wait_send()
 
     early = jnp.logical_not(own_first)
 
     @pl.when(inner)
     def _():
-        own(0).start()
+        send_own(0, (0,))
         share().start()
         passed(0)
-        own_before(1)
+        send_own(1, (0,))
         eig_load.wait()
         near(0)
 
@@ -495,8 +529,11 @@
             apply_local(0, 1, (0,), B)
 
         passed(1)
-        own_after(1)
-        own_before(2)
+
+        @pl.when(own_first)
+        def _():
+            send_own(2, (0,))
+
         far(0)
         near(1)
 
@@ -512,8 +549,16 @@
             straddle(1, (0,), lambda: down_copy(0).start())
 
         passed(2)
-        own_after(2)
-        own_before(3)
+
+        @pl.when(own_first)
+        def _():
+            send_own(3, (0, 1, 2))
+
+        @pl.when(early)
+        def _():
+            send_own(2, (0,))
+            send_own(3, (0,))
+
         far(1)
 
         @pl.when(col == 1)
@@ -555,9 +600,14 @@
             far_even()
 
         columns(1).wait_recv()
+        columns(2).wait_recv()
         apply_local(0, 1, (1,), B)
         straddle(1, (1,), lambda: down_copy(1).start())
-        pass_chunk(3, 0)
+
+        @pl.when(odd == 0)
+        def _():
+            pass_chunk(3, 0)
+
         apply_local(1, 0, (1,), W)
 
         @pl.when(col == 2)
@@ -573,6 +623,11 @@
         def _():
             apply_local(2, 1, (1,), B)
             state(0, B).start()
+
+
+        @pl.when(odd == 1)
+        def _():
+            pass_chunk(3, 0)
 
         pass_chunk(3, 1)
         settle(1)
@@ -588,7 +643,11 @@
             state_up().start()
 
         pass_chunk(3, 2)
-        own_after(3)
+
+        @pl.when(early)
+        def _():
+            send_own(3, (1, 2))
+
 
         @pl.when(own_first)
         def _():
@@ -605,6 +664,7 @@
         def _():
             apply_local(last, 0, (0,), W)
             store(1).start()
+
             far(3)
             straddle(last, (1,), lambda: result(0, back.at[1, 1], down).start())
             result(2, field.at[1, pl.ds(low, W)], row).start()
@@ -624,7 +684,8 @@
         share().wait_send()
         state(0, W).wait_send()
         for s in range(steps):
-            own(s).wait_send()
+            for k in range(own_cuts[s]):
+                own(s, k).wait_send()
             for k in range(cuts[s]):
                 relay(s, k).wait_send()
                 hand(s, k).wait_send()
@@ -686,10 +747,11 @@
         dma = pltpu.SemaphoreType.DMA
         return pl.pallas_call(
             functools.partial(line_kernel, rows_n),
-            out_shape=jax.ShapeDtypeStruct(eigvec.shape, jnp.float32),
-            in_specs=[pl.BlockSpec(memory_space=pltpu.SMEM), anywhere, anywhere, anywhere],
+            out_shape=pltpu.VMEM(eigvec.shape, jnp.float32),
+            in_specs=[anywhere, anywhere, anywhere, anywhere],
             out_specs=anywhere,
             scratch_shapes=[
+                pltpu.SMEM(sched.shape, jnp.int32),
                 pltpu.VMEM(refl.shape, jnp.float32),
                 pltpu.VMEM(tfac.shape, jnp.float32),
                 pltpu.VMEM((2, *eigvec.shape), jnp.float32),
@@ -698,15 +760,15 @@
                 pltpu.VMEM((*two, W, evcount), jnp.float32),
                 pltpu.VMEM((*two, W, evcount), jnp.float32),
                 pltpu.VMEM((2, W, evcount), jnp.float32),
-                dma((2,)),
+                dma((3,)),
                 dma,
                 dma((3,)),
                 dma(chunks),
                 dma(chunks),
-                dma((2,)),
-                dma((2,)),
-                dma((steps,)),
-                dma((steps,)),
+                dma((3,)),
+                dma((3,)),
+                dma(chunks),
+                dma(chunks),
                 dma(chunks),
                 dma(chunks),
                 dma(chunks),
@@ -721,6 +783,7 @@
                 dma,
                 dma((2,)),
                 dma((2,)),
+                pltpu.SemaphoreType.REGULAR,
             ],
             compiler_params=pltpu.CompilerParams(
                 collective_id=0, has_side_effects=True, vmem_limit_bytes=60 << 20

time: 90.7 us -> 87.1 us (0.960)
  Pallas kernels: 88.3 us -> 85.9 us
  local copies, waits for them, and re-layouts: 2.26 us -> 0.97 us
    pallas_call x1, Pallas kernels: 88.3 us -> 85.9 us  [on_device(): pl.pallas_call(functools.partial(line_kernel, rows_n), out_shape=pltpu.VM...]
    unnamed x1, local copies, waits for them, and re-layouts: 2.26 us -> 0.97 us
where the time goes in v2:
time: 87.1 us; the launch traced here: 86.9 us
  Pallas kernels  85.9 us (99%)
  local copies, waits for them, and re-layouts  0.97 us (1%)
    pallas_call x1, Pallas kernels, on_device(): pl.pallas_call(functools.partial(line_kernel, rows_n), out_shape=pltpu.VM...  85.9 us

profile of v2, /device:TPU:0, one launch (start us, length us, event | category | flops | bytes accessed | tf_op | source)
XLA Modules:
  0.0 86.9 jit_solution(17885610887568051630)
XLA Ops:
  0.0 85.9 %sweep.1 = f32[1024,256]{1,0:T(8,128)S(1)} custom-call(s32[2,4]{1,0:T(2,128)} %sched_all.1, f32[4,256,256]{2,1,0:T(8,128)} %refl.1, f32[4,128,256]{2,1,0:T(8,128)} %tfac.1, f32[1024,256]{1,0:T(8,128)} %eig.1), custom_call_target="tpu_custom_call" | custom-call | tf_op jit(solution)/shard_map/sweep/pallas_call | solution.py:748
  86.0 1.0 %copy.6 = f32[1024,256]{1,0:T(8,128)} copy(f32[1024,256]{1,0:T(8,128)S(1)} %sweep.1) | data formatting | bytes 2097152

commit v3 on v2

--- a/solution.py
+++ b/solution.py
@@ -215,9 +215,7 @@
 
 
 def line_kernel(rows_n, sched_all, refl, tfac, eig, out, sched, refl_in, tfac_in, field, buf, fed, inb, back, landed,
-                load_sem, eig_sem, out_sem, feed_send, feed_recv, cols_send, cols_recv, own_send, own_recv,
-                relay_send, relay_recv, hand_send, hand_recv, up_send, up_recv, down_send, down_recv,
-                res_send, res_recv, share_send, share_recv, state_send, state_recv, turn_sem):
+                local, eig_sem, sends, recvs, turn_sem):
     steps, v_rows, _ = refl.shape
     low = B + W
     last = steps - 1
@@ -243,10 +241,10 @@
             device_id=target, device_id_type=MESH,
         )
 
-    refl_load = pltpu.make_async_copy(refl, refl_in, load_sem.at[0])
-    tfac_load = pltpu.make_async_copy(tfac, tfac_in, load_sem.at[1])
+    refl_load = pltpu.make_async_copy(refl, refl_in, local.at[0])
+    tfac_load = pltpu.make_async_copy(tfac, tfac_in, local.at[1])
     eig_load = pltpu.make_async_copy(eig, field.at[0], eig_sem)
-    sched_load = pltpu.make_async_copy(sched_all, sched, load_sem.at[2])
+    sched_load = pltpu.make_async_copy(sched_all, sched, local.at[2])
     sched_load.start()
     refl_load.start()
     tfac_load.start()
@@ -293,49 +291,51 @@
         return pl.ds(k * size, size)
 
     def feed(s, k):
+        slot = sum(cuts[:s]) + k
         return remote(buf.at[s, col, span(s, k)], fed.at[s, span(s, k)],
-                      feed_send.at[s, k], feed_recv.at[s, k], (mate, partner))
+                      sends.at[1 + k if s == last else 0], recvs.at[slot], (mate, partner))
+
+    def feeds():
+        return remote(buf.at[pl.ds(0, last), col], fed.at[pl.ds(0, last)], sends.at[0], recvs.at[0], (mate, partner))
 
     column_rows = ((0, B), (B, W), (B + W, W))
 
     def columns(g):
         rows = pl.ds(*column_rows[g])
-        return remote(eig.at[rows], field.at[1, rows], cols_send.at[g], cols_recv.at[g], (row, partner))
-
-    own_cuts = (1, 1, 1, 3)
-
-    def own_span(s, k):
-        size = piece // own_cuts[s]
-        return pl.ds(k * size, size)
-
-    def own(s, k):
-        part = buf.at[s, col, own_span(s, k)]
-        return remote(part, part, own_send.at[s, k], own_recv.at[s, k], (row, other))
-
-    def own_arrival(s, k):
-        part = buf.at[s, other, own_span(s, k)]
-        return remote(part, part, own_send.at[s, k], own_recv.at[s, k], (row, other))
-
-    def send_own(s, ks):
-        for k in ks:
-            own(s, k).start()
+        return remote(eig.at[rows], field.at[1, rows], sends.at[4 + g], recvs.at[8 + g], (row, partner))
+
+    def own(s):
+        return remote(buf.at[s, col], buf.at[s, col], sends.at[0], recvs.at[11 + s], (row, other))
+
+    def own_arrival(s):
+        return remote(buf.at[s, other], buf.at[s, other], sends.at[0], recvs.at[11 + s], (row, other))
+
+    def own_all():
+        return remote(buf.at[:, col], buf.at[:, col], sends.at[0], recvs.at[11], (row, other))
 
     def relay(s, k):
         return remote(fed.at[s, span(s, k)], buf.at[s, partner, span(s, k)],
-                      relay_send.at[s, k], relay_recv.at[s, k], (mate, other))
-
-    def relay_arrival(s, k):
-        owner = 3 - partner
-        return remote(fed.at[s, span(s, k)], buf.at[s, owner, span(s, k)],
-                      relay_send.at[s, k], relay_recv.at[s, k], (mate, other))
+                      sends.at[1], recvs.at[15 + s], (mate, other))
+
+    def relay_arrival(s):
+        return remote(fed.at[s], buf.at[s, 3 - partner], sends.at[1], recvs.at[15 + s], (mate, other))
+
+    def relay_all():
+        return remote(fed, buf.at[:, partner], sends.at[1], recvs.at[15], (mate, other))
 
     def hand(s, k):
         return remote(fed.at[s, span(s, k)], buf.at[s, partner, span(s, k)],
-                      hand_send.at[s, k], hand_recv.at[s, k], (mate, col))
+                      sends.at[2], recvs.at[19 + s], (mate, col))
+
+    def hand_arrival(s):
+        return remote(fed.at[s], buf.at[s, partner], sends.at[2], recvs.at[19 + s], (mate, col))
+
+    def hand_all():
+        return remote(fed, buf.at[:, partner], sends.at[2], recvs.at[19], (mate, col))
 
     def result(part, src, target_row):
         rows = (pl.ds(0, W), pl.ds(W, B), pl.ds(low, W))[part]
-        return remote(src, out.at[rows], res_send.at[part], res_recv.at[part], (target_row, partner))
+        return remote(src, out.at[rows], sends.at[10 + part], recvs.at[5 + part], (target_row, partner))
 
     def vectors_of(s, g):
         return split(buf[s, 2 * g:2 * g + 2, :v_rows].reshape(B, W))
@@ -362,13 +362,13 @@
         save(zs, start, rows - product(vectors, coeffs, ((1,), (0,))))
 
     def up_copy(i, z):
-        return remote(field.at[z, pl.ds(0, W)], inb.at[i, z], up_send.at[i, z], up_recv.at[i, z], (up, col))
+        return remote(field.at[z, pl.ds(0, W)], inb.at[i, z], sends.at[3 + 2 * i + z], recvs.at[23 + 2 * i + z], (up, col))
 
     def down_copy(z):
-        return remote(back.at[0, z], landed.at[z], down_send.at[0, z], down_recv.at[0, z], (down, col))
+        return remote(back.at[0, z], landed.at[z], sends.at[7 + z], recvs.at[27 + z], (down, col))
 
     def down_final():
-        return remote(back.at[1, 0], out.at[pl.ds(0, W)], down_send.at[1, 0], down_recv.at[1, 0], (down, col))
+        return remote(back.at[1, 0], out.at[pl.ds(0, W)], sends.at[9], recvs.at[29], (down, col))
 
     def send_up(s, zs):
         @pl.when(has_up)
@@ -415,34 +415,36 @@
             pass_chunk(s, k)
 
     def near(s):
-        for k in range(cuts[s]):
-            hand(s, k).wait_recv()
+        hand_arrival(s).wait_recv()
 
     def far(s):
-        for k in range(own_cuts[s]):
-            own_arrival(s, k).wait_recv()
-        for k in range(cuts[s]):
-            relay_arrival(s, k).wait_recv()
+        own_arrival(s).wait_recv()
+        relay_arrival(s).wait_recv()
 
     def store(part):
         rows = (pl.ds(0, W), pl.ds(W, B), pl.ds(low, W))[part]
-        return pltpu.make_async_copy(field.at[0, rows], out.at[rows], out_sem.at[part])
-
-    def share():
-        return remote(buf.at[last, col], buf.at[last, col], share_send, share_recv, (row, partner))
-
-    def share_arrival():
-        return remote(buf.at[last, partner], buf.at[last, partner], share_send, share_recv, (row, partner))
+        return pltpu.make_async_copy(field.at[0, rows], out.at[rows], local.at[part])
+
+    top_row = (col < 2) & (row == 0)
+    share_slot = {last: 0, 0: 1, 2: 2}
+
+    def share(s):
+        part = buf.at[s, col]
+        return remote(part, part, sends.at[13 + share_slot[s]], recvs.at[share_slot[s]], (row, partner))
+
+    def share_arrival(s):
+        part = buf.at[s, partner]
+        return remote(part, part, sends.at[13 + share_slot[s]], recvs.at[share_slot[s]], (row, partner))
 
     def state(part, start):
         rows = pl.ds(start, W)
-        return remote(field.at[1, rows], field.at[0, rows], state_send.at[part], state_recv.at[part], (row, partner))
+        return remote(field.at[1, rows], field.at[0, rows], sends.at[16 + part], recvs.at[3 + part], (row, partner))
 
     def state_up():
-        return remote(field.at[1, pl.ds(0, W)], inb.at[1, 0], state_send.at[1], state_recv.at[1], (up, partner))
+        return remote(field.at[1, pl.ds(0, W)], inb.at[1, 0], sends.at[17], recvs.at[4], (up, partner))
 
     def bottom_result():
-        return remote(back.at[1, 0], out.at[pl.ds(0, W)], res_send.at[0], res_recv.at[0], (down, col))
+        return remote(back.at[1, 0], out.at[pl.ds(0, W)], sends.at[10], recvs.at[5], (down, col))
 
     @pl.when(jnp.logical_not(inner))
     def _():
@@ -454,36 +456,97 @@
                 feed(k, c).start()
         columns(0).start()
 
+        def wait_turn():
+            pl.semaphore_wait(turn_sem, 1)
+
+        def last_feed():
+            for c in range(cuts[last]):
+                feed(last, c).start()
+
+        feeds_first = (col == 0) == (odd == 0)
+
         @pl.when(odd == 0)
         def _():
-            pl.semaphore_wait(turn_sem, 1)
+            wait_turn()
 
         columns(1).start()
         columns(2).start()
         columns(1).wait_send()
 
+        @pl.when(odd == 1)
+        def _():
+            turn()
+
+            @pl.when(feeds_first)
+            def _():
+                wait_turn()
+
+            columns(2).wait_send()
+
         @pl.when(odd == 0)
         def _():
+            @pl.when(feeds_first)
+            def _():
+                last_feed()
+
             columns(2).wait_send()
 
-        turn()
-
-        @pl.when(odd == 1)
-        def _():
-            pl.semaphore_wait(turn_sem, 1)
-            columns(2).wait_send()
-
-        for c in range(cuts[last]):
-            feed(last, c).start()
-        share_arrival().wait_recv()
+            @pl.when(jnp.logical_not(feeds_first))
+            def _():
+                turn()
+
+        @pl.when(feeds_first)
+        def _():
+            @pl.when(odd == 1)
+            def _():
+                last_feed()
+
+            feed(last, 1).wait_send()
+            turn()
+            feed(last, 0).wait_send()
+            feed(last, 2).wait_send()
+
+        @pl.when(jnp.logical_not(feeds_first))
+        def _():
+            wait_turn()
+            last_feed()
+            for c in range(cuts[last]):
+                feed(last, c).wait_send()
+
+        share_arrival(last).wait_recv()
+
+        @pl.when(top_row)
+        def _():
+            share_arrival(0).wait_recv()
+            share_arrival(2).wait_recv()
+            top_load = pltpu.make_async_copy(eig.at[pl.ds(0, B)], field.at[1, pl.ds(0, B)], eig_sem)
+            top_load.start()
+            top_load.wait()
+            apply_local(0, 0, (1,), 0)
+            field[0, :W] = field[1, :W]
+            state(1, W).wait_recv()
+            apply_local(2, 0, (0,), 0)
+            store(0).start()
+
         state(0, W).wait_recv()
 
         @pl.when(col == 0)
         def _():
-            state(1, W).wait_recv()
+            @pl.when(has_up)
+            def _():
+                state(1, W).wait_recv()
+
             apply_local(last, 0, (0,), W)
             store(1).start()
-            result(0, field.at[0, pl.ds(0, W)], row).wait_recv()
+
+            @pl.when(has_up)
+            def _():
+                result(0, field.at[0, pl.ds(0, W)], row).wait_recv()
+
+            @pl.when(jnp.logical_not(has_up))
+            def _():
+                store(0).wait()
+
             result(2, field.at[0, pl.ds(0, W)], row).wait_recv()
             store(1).wait()
 
@@ -503,19 +566,16 @@
             def _():
                 bottom_result().wait_send()
 
-        for s in range(steps):
-            for k in range(cuts[s]):
-                feed(s, k).wait_send()
+        feeds().wait_send()
         columns(0).wait_send()
 
     early = jnp.logical_not(own_first)
 
     @pl.when(inner)
     def _():
-        send_own(0, (0,))
-        share().start()
+        own(0).start()
         passed(0)
-        send_own(1, (0,))
+        own(1).start()
         eig_load.wait()
         near(0)
 
@@ -529,10 +589,17 @@
             apply_local(0, 1, (0,), B)
 
         passed(1)
+        share(last).start()
+
+        @pl.when(top_row)
+        def _():
+            share(0).start()
+            share(2).start()
+
 
         @pl.when(own_first)
         def _():
-            send_own(2, (0,))
+            own(2).start()
 
         far(0)
         near(1)
@@ -552,12 +619,11 @@
 
         @pl.when(own_first)
         def _():
-            send_own(3, (0, 1, 2))
+            own(3).start()
 
         @pl.when(early)
         def _():
-            send_own(2, (0,))
-            send_own(3, (0,))
+            own(2).start()
 
         far(1)
 
@@ -604,11 +670,23 @@
         apply_local(0, 1, (1,), B)
         straddle(1, (1,), lambda: down_copy(1).start())
 
-        @pl.when(odd == 0)
+        @pl.when(early & (odd == 0))
         def _():
             pass_chunk(3, 0)
 
         apply_local(1, 0, (1,), W)
+
+        @pl.when(top_row)
+        def _():
+            state(1, W).start()
+
+        @pl.when(early & (odd == 1))
+        def _():
+            pass_chunk(3, 0)
+
+        @pl.when(early & (odd == 0))
+        def _():
+            pass_chunk(3, 1)
 
         @pl.when(col == 2)
         def _():
@@ -625,70 +703,102 @@
             state(0, B).start()
 
 
-        @pl.when(odd == 1)
-        def _():
-            pass_chunk(3, 0)
-
-        pass_chunk(3, 1)
+        @pl.when(early & (odd == 1))
+        def _():
+            pass_chunk(3, 1)
+
         settle(1)
-        apply_local(2, 0, (1,), 0)
+
+        @pl.when(early)
+        def _():
+            pass_chunk(3, 2)
+            own(3).start()
+
+        @pl.when(jnp.logical_not(top_row))
+        def _():
+            apply_local(2, 0, (1,), 0)
+
+        @pl.when((col == 1) & has_up)
+        def _():
+            state(1, W).start()
+            up_copy(1, 1).start()
+
+        @pl.when((col == 2) & has_up)
+        def _():
+            state_up().start()
+
+
+        @pl.when(own_first)
+        def _():
+            passed(3)
+
+
+        @pl.when(own_first)
+        def _():
+            far_even()
+
+        @pl.when(jnp.logical_not(has_up))
+        def _():
+            store(0).start()
+
+        @pl.when((col == 2) & jnp.logical_not(has_up))
+        def _():
+            result(0, field.at[1, pl.ds(0, W)], row).start()
+
+        def near_last():
+            near(3)
+
+            @pl.when(col == 1)
+            def _():
+                apply_local(last, 0, (0,), W)
+                store(1).start()
+
+            @pl.when(col == 2)
+            def _():
+                straddle(last, (0,), lambda: down_final().start())
+                store(2).start()
+
+        @pl.when(own_first)
+        def _():
+            near_last()
+
+        far(3)
 
         @pl.when(col == 1)
         def _():
-            state(1, W).start()
-            send_up(2, (1,))
-
-        @pl.when((col == 2) & has_up)
-        def _():
-            state_up().start()
-
-        pass_chunk(3, 2)
+            straddle(last, (1,), lambda: result(0, back.at[1, 1], down).start())
+            result(2, field.at[1, pl.ds(low, W)], row).start()
+
+        @pl.when(col == 2)
+        def _():
+            apply_local(last, 0, (1,), W)
+            result(1, field.at[1, pl.ds(W, B)], row).start()
 
         @pl.when(early)
         def _():
-            send_own(3, (1, 2))
-
-
-        @pl.when(own_first)
-        def _():
-            far_even()
-
-        @pl.when(jnp.logical_not(has_up))
-        def _():
-            result(0, field.at[1, pl.ds(0, W)], row).start()
-            store(0).start()
-
-        near(3)
+            near_last()
 
         @pl.when(col == 1)
+        def _():
+            straddle(last, (0,), lambda: down_final().start())
+            store(2).start()
+
+        @pl.when(col == 2)
         def _():
             apply_local(last, 0, (0,), W)
             store(1).start()
 
-            far(3)
-            straddle(last, (1,), lambda: result(0, back.at[1, 1], down).start())
-            result(2, field.at[1, pl.ds(low, W)], row).start()
-            straddle(last, (0,), lambda: down_final().start())
-            store(2).start()
-
-        @pl.when(col == 2)
-        def _():
-            straddle(last, (0,), lambda: down_final().start())
-            store(2).start()
-            far(3)
-            apply_local(last, 0, (1,), W)
-            result(1, field.at[1, pl.ds(W, B)], row).start()
-            apply_local(last, 0, (0,), W)
-            store(1).start()
-
-        share().wait_send()
+        share(last).wait_send()
+
+        @pl.when(top_row)
+        def _():
+            share(0).wait_send()
+            share(2).wait_send()
+
         state(0, W).wait_send()
-        for s in range(steps):
-            for k in range(own_cuts[s]):
-                own(s, k).wait_send()
-            for k in range(cuts[s]):
-                relay(s, k).wait_send()
-                hand(s, k).wait_send()
+        own_all().wait_send()
+        relay_all().wait_send()
+        hand_all().wait_send()
 
         @pl.when(has_up)
         def _():
@@ -703,7 +813,6 @@
 
         @pl.when(jnp.logical_not(has_up))
         def _():
-            result(0, field.at[1, pl.ds(0, W)], row).wait_send()
             store(0).wait()
 
         @pl.when(col == 1)
@@ -725,6 +834,10 @@
             @pl.when(has_up)
             def _():
                 state_up().wait_send()
+
+            @pl.when(jnp.logical_not(has_up))
+            def _():
+                result(0, field.at[1, pl.ds(0, W)], row).wait_send()
 
             result(1, field.at[1, pl.ds(W, B)], row).wait_send()
 
@@ -743,7 +856,6 @@
     anywhere = pl.BlockSpec(memory_space=pl.ANY)
     if n == 4 and groups == 2 and steps == 4 and rows_n % 2 == 0:
         two = (half_steps, 2)
-        chunks = (steps, 3)
         dma = pltpu.SemaphoreType.DMA
         return pl.pallas_call(
             functools.partial(line_kernel, rows_n),
@@ -762,27 +874,8 @@
                 pltpu.VMEM((2, W, evcount), jnp.float32),
                 dma((3,)),
                 dma,
-                dma((3,)),
-                dma(chunks),
-                dma(chunks),
-                dma((3,)),
-                dma((3,)),
-                dma(chunks),
-                dma(chunks),
-                dma(chunks),
-                dma(chunks),
-                dma(chunks),
-                dma(chunks),
-                dma(two),
-                dma(two),
-                dma(two),
-                dma(two),
-                dma((3,)),
-                dma((3,)),
-                dma,
-                dma,
-                dma((2,)),
-                dma((2,)),
+                dma((18,)),
+                dma((30,)),
                 pltpu.SemaphoreType.REGULAR,
             ],
             compiler_params=pltpu.CompilerParams(

time: 87.1 us -> 85.1 us (0.977)
  Pallas kernels: 85.9 us -> 83.9 us
    pallas_call x1, Pallas kernels: 85.9 us -> 83.9 us  [on_device(): pl.pallas_call(functools.partial(line_kernel, rows_n), out_shape=pltpu.VM...]
where the time goes in v3:
time: 85.1 us; the launch traced here: 84.9 us
  Pallas kernels  83.9 us (99%)
  local copies, waits for them, and re-layouts  0.97 us (1%)
    pallas_call x1, Pallas kernels, on_device(): pl.pallas_call(functools.partial(line_kernel, rows_n), out_shape=pltpu.VM...  83.9 us

profile of v3, /device:TPU:0, one launch (start us, length us, event | category | flops | bytes accessed | tf_op | source)
XLA Modules:
  0.0 84.9 jit_solution(17950763093856463559)
XLA Ops:
  0.0 83.9 %sweep.1 = f32[1024,256]{1,0:T(8,128)S(1)} custom-call(s32[2,4]{1,0:T(2,128)} %sched_all.1, f32[4,256,256]{2,1,0:T(8,128)} %refl.1, f32[4,128,256]{2,1,0:T(8,128)} %tfac.1, f32[1024,256]{1,0:T(8,128)} %eig.1), custom_call_target="tpu_custom_call" | custom-call | tf_op jit(solution)/shard_map/sweep/pallas_call | solution.py:860
  83.9 1.0 %copy.6 = f32[1024,256]{1,0:T(8,128)} copy(f32[1024,256]{1,0:T(8,128)S(1)} %sweep.1) | data formatting | bytes 2097152

commit v4 on v3

--- a/solution.py
+++ b/solution.py
@@ -229,7 +229,8 @@
     beyond = row - 1 + 2 * odd
     has_beyond = (beyond >= 0) & (beyond < rows_n)
     beyond = jnp.clip(beyond, 0, rows_n - 1)
-    own_first = (col == 1) == (odd == 0)
+    early = odd == 0
+    late = odd == 1
     has_down = row < rows_n - 1
     has_up = row > 0
     down = jnp.minimum(row + 1, rows_n - 1)
@@ -463,9 +464,7 @@
             for c in range(cuts[last]):
                 feed(last, c).start()
 
-        feeds_first = (col == 0) == (odd == 0)
-
-        @pl.when(odd == 0)
+        @pl.when(early)
         def _():
             wait_turn()
 
@@ -473,46 +472,26 @@
         columns(2).start()
         columns(1).wait_send()
 
-        @pl.when(odd == 1)
+        @pl.when(late)
         def _():
             turn()
-
-            @pl.when(feeds_first)
-            def _():
-                wait_turn()
-
             columns(2).wait_send()
-
-        @pl.when(odd == 0)
-        def _():
-            @pl.when(feeds_first)
-            def _():
-                last_feed()
-
+            wait_turn()
+
+        last_feed()
+
+        @pl.when(early)
+        def _():
             columns(2).wait_send()
 
-            @pl.when(jnp.logical_not(feeds_first))
-            def _():
-                turn()
-
-        @pl.when(feeds_first)
-        def _():
-            @pl.when(odd == 1)
-            def _():
-                last_feed()
-
-            feed(last, 1).wait_send()
+        feed(last, 0).wait_send()
+        feed(last, 1).wait_send()
+
+        @pl.when(early)
+        def _():
             turn()
-            feed(last, 0).wait_send()
-            feed(last, 2).wait_send()
-
-        @pl.when(jnp.logical_not(feeds_first))
-        def _():
-            wait_turn()
-            last_feed()
-            for c in range(cuts[last]):
-                feed(last, c).wait_send()
-
+
+        feed(last, 2).wait_send()
         share_arrival(last).wait_recv()
 
         @pl.when(top_row)
@@ -569,8 +548,6 @@
         feeds().wait_send()
         columns(0).wait_send()
 
-    early = jnp.logical_not(own_first)
-
     @pl.when(inner)
     def _():
         own(0).start()
@@ -597,7 +574,7 @@
             share(2).start()
 
 
-        @pl.when(own_first)
+        @pl.when(early)
         def _():
             own(2).start()
 
@@ -617,11 +594,11 @@
 
         passed(2)
 
-        @pl.when(own_first)
+        @pl.when(early)
         def _():
             own(3).start()
 
-        @pl.when(early)
+        @pl.when(late)
         def _():
             own(2).start()
 
@@ -670,30 +647,22 @@
         apply_local(0, 1, (1,), B)
         straddle(1, (1,), lambda: down_copy(1).start())
 
-        @pl.when(early & (odd == 0))
+        apply_local(1, 0, (1,), W)
+
+        @pl.when(top_row)
+        def _():
+            state(1, W).start()
+
+        @pl.when(late)
         def _():
             pass_chunk(3, 0)
-
-        apply_local(1, 0, (1,), W)
-
-        @pl.when(top_row)
-        def _():
-            state(1, W).start()
-
-        @pl.when(early & (odd == 1))
-        def _():
-            pass_chunk(3, 0)
-
-        @pl.when(early & (odd == 0))
-        def _():
-            pass_chunk(3, 1)
 
         @pl.when(col == 2)
         def _():
             apply_local(2, 1, (1,), B)
             state(0, low).start()
 
-        @pl.when(own_first)
+        @pl.when(late)
         def _():
             far(2)
 
@@ -703,13 +672,13 @@
             state(0, B).start()
 
 
-        @pl.when(early & (odd == 1))
+        @pl.when(late)
         def _():
             pass_chunk(3, 1)
 
         settle(1)
 
-        @pl.when(early)
+        @pl.when(late)
         def _():
             pass_chunk(3, 2)
             own(3).start()
@@ -728,12 +697,12 @@
             state_up().start()
 
 
-        @pl.when(own_first)
+        @pl.when(early)
         def _():
             passed(3)
 
 
-        @pl.when(own_first)
+        @pl.when(late)
         def _():
             far_even()
 
@@ -758,7 +727,7 @@
                 straddle(last, (0,), lambda: down_final().start())
                 store(2).start()
 
-        @pl.when(own_first)
+        @pl.when(late)
         def _():
             near_last()
 

time: 85.1 us -> 83.6 us (0.982)
  the two profiles are of different devices: /device:TPU:0 before, /device:TPU:3 now
where the time goes in v4:
time: 83.6 us; the launch traced here: 83.4 us
  Pallas kernels  82.4 us (99%)
  local copies, waits for them, and re-layouts  0.97 us (1%)
    pallas_call x1, Pallas kernels, on_device(): pl.pallas_call(functools.partial(line_kernel, rows_n), out_shape=pltpu.VM...  82.4 us

profile of v4, /device:TPU:3, one launch (start us, length us, event | category | flops | bytes accessed | tf_op | source)
XLA Modules:
  0.0 83.4 jit_solution(13568585823975150844)
XLA Ops:
  0.0 82.4 %sweep.1 = f32[1024,256]{1,0:T(8,128)S(1)} custom-call(s32[2,4]{1,0:T(2,128)} %sched_all.1, f32[4,256,256]{2,1,0:T(8,128)} %refl.1, f32[4,128,256]{2,1,0:T(8,128)} %tfac.1, f32[1024,256]{1,0:T(8,128)} %eig.1), custom_call_target="tpu_custom_call" | custom-call | tf_op jit(solution)/shard_map/sweep/pallas_call | solution.py:829
  82.4 1.0 %copy.6 = f32[1024,256]{1,0:T(8,128)} copy(f32[1024,256]{1,0:T(8,128)S(1)} %sweep.1) | data formatting | bytes 2097152

commit v5 on v4

--- a/solution.py
+++ b/solution.py
@@ -273,15 +273,13 @@
     refl_load.wait()
     tfac_load.wait()
 
-    @pl.when(inner)
-    def _():
-        eig_load.start()
-
-    for s in range(steps):
+    def pick(s):
         slot = sched[col // 2, s]
         buf[s, col, :v_rows] = refl_in[slot]
         buf[s, col, v_rows:] = tfac_in[slot]
 
+    pick(0)
+
     pl.semaphore_wait(barrier, 3 + 2 * has_beyond.astype(jnp.int32) + 2 * inner.astype(jnp.int32))
 
     cuts = (3, 1, 1, 3)
@@ -289,7 +287,7 @@
 
     def span(s, k):
         size = piece // cuts[s]
-        return pl.ds(k * size, size)
+        return pl.ds((k + 2) % 3 * size if s == last else k * size, size)
 
     def feed(s, k):
         slot = sum(cuts[:s]) + k
@@ -305,18 +303,38 @@
         rows = pl.ds(*column_rows[g])
         return remote(eig.at[rows], field.at[1, rows], sends.at[4 + g], recvs.at[8 + g], (row, partner))
 
+    lead = piece // 3
+
     def own(s):
         return remote(buf.at[s, col], buf.at[s, col], sends.at[0], recvs.at[11 + s], (row, other))
 
     def own_arrival(s):
         return remote(buf.at[s, other], buf.at[s, other], sends.at[0], recvs.at[11 + s], (row, other))
 
+    def own_last(k, owner):
+        part = buf.at[last, owner, (pl.ds(lead, piece - lead), pl.ds(0, lead))[k]]
+        return remote(part, part, sends.at[0], recvs.at[(11 + last, 30)[k]], (row, other))
+
+    def send_last():
+        own_last(0, col).start()
+        own_last(1, col).start()
+
     def own_all():
         return remote(buf.at[:, col], buf.at[:, col], sends.at[0], recvs.at[11], (row, other))
 
     def relay(s, k):
         return remote(fed.at[s, span(s, k)], buf.at[s, partner, span(s, k)],
-                      sends.at[1], recvs.at[15 + s], (mate, other))
+                      sends.at[1], recvs.at[31 if s == last and k == 2 else 15 + s], (mate, other))
+
+    def relay_end():
+        rows = pl.ds(lead, lead)
+        return remote(fed.at[last, rows], buf.at[last, 3 - partner, rows],
+                      sends.at[1], recvs.at[31], (mate, other))
+
+    def relay_lead():
+        rows = pl.ds(0, 2 * lead)
+        return remote(fed.at[last, rows], buf.at[last, 3 - partner, rows],
+                      sends.at[1], recvs.at[15 + last], (mate, other))
 
     def relay_arrival(s):
         return remote(fed.at[s], buf.at[s, 3 - partner], sends.at[1], recvs.at[15 + s], (mate, other))
@@ -422,6 +440,14 @@
         own_arrival(s).wait_recv()
         relay_arrival(s).wait_recv()
 
+    def far_lead():
+        own_last(0, other).wait_recv()
+        relay_lead().wait_recv()
+
+    def far_end():
+        own_last(1, other).wait_recv()
+        relay_end().wait_recv()
+
     def store(part):
         rows = (pl.ds(0, W), pl.ds(W, B), pl.ds(low, W))[part]
         return pltpu.make_async_copy(field.at[0, rows], out.at[rows], local.at[part])
@@ -436,6 +462,51 @@
     def share_arrival(s):
         part = buf.at[s, partner]
         return remote(part, part, sends.at[13 + share_slot[s]], recvs.at[share_slot[s]], (row, partner))
+
+    def half_result(part, half):
+        start = (0, None, low)[part] + half * lead
+        src = back.at[1, 1, pl.ds(half * lead, lead)] if part == 0 else field.at[1, pl.ds(start, lead)]
+        return remote(src, out.at[pl.ds(start, lead)], sends.at[10 + part], recvs.at[5 + part],
+                      (down if part == 0 else row, partner))
+
+    def rows_of(owner, start):
+        return split(buf[last, owner, start:start + lead])
+
+    def joined(a, b):
+        return jnp.concatenate([a[0], b[0]], axis=0), jnp.concatenate([a[1], b[1]], axis=0)
+
+    def late_straddle():
+        far_lead()
+
+        @pl.when(jnp.logical_not(has_down))
+        def _():
+            far_end()
+            half_result(2, 0).start()
+            half_result(2, 1).start()
+
+        @pl.when(has_down)
+        def _():
+            up_copy(1, 1).wait_recv()
+            factor = factor_of(last, 1)
+            inside = joined(rows_of(2, lead), rows_of(3, 0))
+            rows_in = jnp.concatenate([field[1, low + lead:low + W], inb[1, 1, :lead]], axis=0)
+            rows_out = jnp.concatenate([field[1, low:low + lead], inb[1, 1, lead:]], axis=0)
+            part = product(inside, split(rows_in), ((0,), (0,)))
+            scaled = split(product(inside, factor, ((1,), (0,))))
+            far_end()
+            outside = joined(rows_of(2, 0), rows_of(3, lead))
+            coupling = split(part + product(outside, split(rows_out), ((0,), (0,))))
+            value = rows_in - product(scaled, coupling, ((1,), (0,)))
+            back[1, 1, :lead] = value[lead:]
+            field[1, low + lead:low + W] = value[:lead]
+            half_result(0, 0).start()
+            half_result(2, 1).start()
+            ends = split(product(outside, factor, ((1,), (0,))))
+            value = rows_out - product(ends, coupling, ((1,), (0,)))
+            back[1, 1, lead:] = value[lead:]
+            field[1, low:low + lead] = value[:lead]
+            half_result(0, 1).start()
+            half_result(2, 0).start()
 
     def state(part, start):
         rows = pl.ds(start, W)
@@ -453,9 +524,12 @@
             pl.semaphore_signal(turn_sem, inc=1, device_id=(mate, col), device_id_type=MESH)
 
         for k in range(last):
+            if k > 0:
+                pick(k)
             for c in range(cuts[k]):
                 feed(k, c).start()
         columns(0).start()
+        pick(last)
 
         def wait_turn():
             pl.semaphore_wait(turn_sem, 1)
@@ -464,7 +538,7 @@
             for c in range(cuts[last]):
                 feed(last, c).start()
 
-        @pl.when(early)
+        @pl.when(late)
         def _():
             wait_turn()
 
@@ -472,18 +546,19 @@
         columns(2).start()
         columns(1).wait_send()
 
-        @pl.when(late)
+        @pl.when(early)
         def _():
             turn()
             columns(2).wait_send()
             wait_turn()
 
+        @pl.when(late)
+        def _():
+            columns(2).wait_send()
+            turn()
+            wait_turn()
+
         last_feed()
-
-        @pl.when(early)
-        def _():
-            columns(2).wait_send()
-
         feed(last, 0).wait_send()
         feed(last, 1).wait_send()
 
@@ -551,6 +626,9 @@
     @pl.when(inner)
     def _():
         own(0).start()
+        eig_load.start()
+        for s in range(1, steps):
+            pick(s)
         passed(0)
         own(1).start()
         eig_load.wait()
@@ -596,7 +674,7 @@
 
         @pl.when(early)
         def _():
-            own(3).start()
+            send_last()
 
         @pl.when(late)
         def _():
@@ -681,7 +759,7 @@
         @pl.when(late)
         def _():
             pass_chunk(3, 2)
-            own(3).start()
+            send_last()
 
         @pl.when(jnp.logical_not(top_row))
         def _():
@@ -731,12 +809,19 @@
         def _():
             near_last()
 
-        far(3)
-
-        @pl.when(col == 1)
+        @pl.when(early | (col == 2))
+        def _():
+            far_lead()
+            far_end()
+
+        @pl.when((col == 1) & early)
         def _():
             straddle(last, (1,), lambda: result(0, back.at[1, 1], down).start())
             result(2, field.at[1, pl.ds(low, W)], row).start()
+
+        @pl.when((col == 1) & late)
+        def _():
+            late_straddle()
 
         @pl.when(col == 2)
         def _():
@@ -844,7 +929,7 @@
                 dma((3,)),
                 dma,
                 dma((18,)),
-                dma((30,)),
+                dma((32,)),
                 pltpu.SemaphoreType.REGULAR,
             ],
             compiler_params=pltpu.CompilerParams(

time: 83.6 us -> 83.5 us (level); the launches traced: 83.4 us -> 82.1 us
  Pallas kernels: 82.4 us -> 81.2 us
    pallas_call x1, Pallas kernels: 82.4 us -> 81.2 us  [on_device(): pl.pallas_call(functools.partial(line_kernel, rows_n), out_shape=pltpu.VM...]
where the time goes in v5:
time: 83.5 us; the launch traced here: 82.1 us
  Pallas kernels  81.2 us (97%)
  local copies, waits for them, and re-layouts  0.97 us (1%)
    pallas_call x1, Pallas kernels, on_device(): pl.pallas_call(functools.partial(line_kernel, rows_n), out_shape=pltpu.VM...  81.2 us

profile of v5, /device:TPU:3, one launch (start us, length us, event | category | flops | bytes accessed | tf_op | source)
XLA Modules:
  0.0 82.1 jit_solution(10521797673328472173)
XLA Ops:
  0.0 81.2 %sweep.1 = f32[1024,256]{1,0:T(8,128)S(1)} custom-call(s32[2,4]{1,0:T(2,128)} %sched_all.1, f32[4,256,256]{2,1,0:T(8,128)} %refl.1, f32[4,128,256]{2,1,0:T(8,128)} %tfac.1, f32[1024,256]{1,0:T(8,128)} %eig.1), custom_call_target="tpu_custom_call" | custom-call | tf_op jit(solution)/shard_map/sweep/pallas_call | solution.py:914
  81.2 1.0 %copy.6 = f32[1024,256]{1,0:T(8,128)} copy(f32[1024,256]{1,0:T(8,128)S(1)} %sweep.1) | data formatting | bytes 2097152

commit v6 on v5

--- a/solution.py
+++ b/solution.py
@@ -499,14 +499,27 @@
             value = rows_in - product(scaled, coupling, ((1,), (0,)))
             back[1, 1, :lead] = value[lead:]
             field[1, low + lead:low + W] = value[:lead]
-            half_result(0, 0).start()
+
+            @pl.when(row != 1)
+            def _():
+                half_result(0, 0).start()
+
             half_result(2, 1).start()
             ends = split(product(outside, factor, ((1,), (0,))))
             value = rows_out - product(ends, coupling, ((1,), (0,)))
             back[1, 1, lead:] = value[lead:]
             field[1, low:low + lead] = value[:lead]
-            half_result(0, 1).start()
-            half_result(2, 0).start()
+
+            @pl.when(row == 1)
+            def _():
+                half_result(2, 0).start()
+                half_result(0, 0).start()
+                half_result(0, 1).start()
+
+            @pl.when(row != 1)
+            def _():
+                half_result(0, 1).start()
+                half_result(2, 0).start()
 
     def state(part, start):
         rows = pl.ds(start, W)

time: 83.5 us -> 82.7 us (level); the launches traced: 82.1 us -> 82.4 us
  no operation moved by 1% of the time
where the time goes in v6:
time: 82.7 us; the launch traced here: 82.4 us
  Pallas kernels  81.4 us (98%)
  local copies, waits for them, and re-layouts  0.97 us (1%)
    pallas_call x1, Pallas kernels, on_device(): pl.pallas_call(functools.partial(line_kernel, rows_n), out_shape=pltpu.VM...  81.4 us

profile of v6, /device:TPU:3, one launch (start us, length us, event | category | flops | bytes accessed | tf_op | source)
XLA Modules:
  0.0 82.4 jit_solution(5588503724155328543)
XLA Ops:
  0.0 81.4 %sweep.1 = f32[1024,256]{1,0:T(8,128)S(1)} custom-call(s32[2,4]{1,0:T(2,128)} %sched_all.1, f32[4,256,256]{2,1,0:T(8,128)} %refl.1, f32[4,128,256]{2,1,0:T(8,128)} %tfac.1, f32[1024,256]{1,0:T(8,128)} %eig.1), custom_call_target="tpu_custom_call" | custom-call | tf_op jit(solution)/shard_map/sweep/pallas_call | solution.py:927
  81.5 1.0 %copy.6 = f32[1024,256]{1,0:T(8,128)} copy(f32[1024,256]{1,0:T(8,128)S(1)} %sweep.1) | data formatting | bytes 2097152

commit v7 on v6

--- a/solution.py
+++ b/solution.py
@@ -282,7 +282,7 @@
 
     pl.semaphore_wait(barrier, 3 + 2 * has_beyond.astype(jnp.int32) + 2 * inner.astype(jnp.int32))
 
-    cuts = (3, 1, 1, 3)
+    cuts = (2, 2, 1, 3)
     piece = buf.shape[2]
 
     def span(s, k):
@@ -381,7 +381,7 @@
         save(zs, start, rows - product(vectors, coeffs, ((1,), (0,))))
 
     def up_copy(i, z):
-        return remote(field.at[z, pl.ds(0, W)], inb.at[i, z], sends.at[3 + 2 * i + z], recvs.at[23 + 2 * i + z], (up, col))
+        return remote(field.at[z, pl.ds(0, W)], inb.at[i, z], sends.at[3 + z], recvs.at[23 + z], (up, col))
 
     def down_copy(z):
         return remote(back.at[0, z], landed.at[z], sends.at[7 + z], recvs.at[27 + z], (down, col))

time: 82.7 us -> 82.7 us (level)
  no operation moved by 1% of the time
where the time goes in v7:
time: 82.7 us; the launch traced here: 82.4 us
  Pallas kernels  81.4 us (98%)
  local copies, waits for them, and re-layouts  0.97 us (1%)
    pallas_call x1, Pallas kernels, on_device(): pl.pallas_call(functools.partial(line_kernel, rows_n), out_shape=pltpu.VM...  81.4 us

profile of v7, /device:TPU:3, one launch (start us, length us, event | category | flops | bytes accessed | tf_op | source)
XLA Modules:
  0.0 82.4 jit_solution(13457403329673538818)
XLA Ops:
  0.0 81.4 %sweep.1 = f32[1024,256]{1,0:T(8,128)S(1)} custom-call(s32[2,4]{1,0:T(2,128)} %sched_all.1, f32[4,256,256]{2,1,0:T(8,128)} %refl.1, f32[4,128,256]{2,1,0:T(8,128)} %tfac.1, f32[1024,256]{1,0:T(8,128)} %eig.1), custom_call_target="tpu_custom_call" | custom-call | tf_op jit(solution)/shard_map/sweep/pallas_call | solution.py:927
  81.5 1.0 %copy.6 = f32[1024,256]{1,0:T(8,128)} copy(f32[1024,256]{1,0:T(8,128)S(1)} %sweep.1) | data formatting | bytes 2097152

commit v8 on v7

--- a/solution.py
+++ b/solution.py
@@ -313,7 +313,7 @@
 
     def own_last(k, owner):
         part = buf.at[last, owner, (pl.ds(lead, piece - lead), pl.ds(0, lead))[k]]
-        return remote(part, part, sends.at[0], recvs.at[(11 + last, 30)[k]], (row, other))
+        return remote(part, part, sends.at[0], recvs.at[(11 + last, 25)[k]], (row, other))
 
     def send_last():
         own_last(0, col).start()
@@ -324,12 +324,12 @@
 
     def relay(s, k):
         return remote(fed.at[s, span(s, k)], buf.at[s, partner, span(s, k)],
-                      sends.at[1], recvs.at[31 if s == last and k == 2 else 15 + s], (mate, other))
+                      sends.at[1], recvs.at[26 if s == last and k == 2 else 15 + s], (mate, other))
 
     def relay_end():
         rows = pl.ds(lead, lead)
         return remote(fed.at[last, rows], buf.at[last, 3 - partner, rows],
-                      sends.at[1], recvs.at[31], (mate, other))
+                      sends.at[1], recvs.at[26], (mate, other))
 
     def relay_lead():
         rows = pl.ds(0, 2 * lead)
@@ -457,11 +457,11 @@
 
     def share(s):
         part = buf.at[s, col]
-        return remote(part, part, sends.at[13 + share_slot[s]], recvs.at[share_slot[s]], (row, partner))
+        return remote(part, part, sends.at[13 if s == last else 2 + share_slot[s]], recvs.at[share_slot[s]], (row, partner))
 
     def share_arrival(s):
         part = buf.at[s, partner]
-        return remote(part, part, sends.at[13 + share_slot[s]], recvs.at[share_slot[s]], (row, partner))
+        return remote(part, part, sends.at[13 if s == last else 2 + share_slot[s]], recvs.at[share_slot[s]], (row, partner))
 
     def half_result(part, half):
         start = (0, None, low)[part] + half * lead
@@ -523,10 +523,10 @@
 
     def state(part, start):
         rows = pl.ds(start, W)
-        return remote(field.at[1, rows], field.at[0, rows], sends.at[16 + part], recvs.at[3 + part], (row, partner))
+        return remote(field.at[1, rows], field.at[0, rows], sends.at[5 + part], recvs.at[3 + part], (row, partner))
 
     def state_up():
-        return remote(field.at[1, pl.ds(0, W)], inb.at[1, 0], sends.at[17], recvs.at[4], (up, partner))
+        return remote(field.at[1, pl.ds(0, W)], inb.at[1, 0], sends.at[6], recvs.at[4], (up, partner))
 
     def bottom_result():
         return remote(back.at[1, 0], out.at[pl.ds(0, W)], sends.at[10], recvs.at[5], (down, col))
@@ -941,8 +941,8 @@
                 pltpu.VMEM((2, W, evcount), jnp.float32),
                 dma((3,)),
                 dma,
-                dma((18,)),
-                dma((32,)),
+                dma((14,)),
+                dma((30,)),
                 pltpu.SemaphoreType.REGULAR,
             ],
             compiler_params=pltpu.CompilerParams(

time: 82.7 us -> 82.6 us (level)
  no operation moved by 1% of the time
where the time goes in v8:
time: 82.6 us; the launch traced here: 82.4 us
  Pallas kernels  81.4 us (99%)
  local copies, waits for them, and re-layouts  0.97 us (1%)
    pallas_call x1, Pallas kernels, on_device(): pl.pallas_call(functools.partial(line_kernel, rows_n), out_shape=pltpu.VM...  81.4 us

profile of v8, /device:TPU:3, one launch (start us, length us, event | category | flops | bytes accessed | tf_op | source)
XLA Modules:
  0.0 82.4 jit_solution(821403416467222126)
XLA Ops:
  0.0 81.4 %sweep.1 = f32[1024,256]{1,0:T(8,128)S(1)} custom-call(s32[2,4]{1,0:T(2,128)} %sched_all.1, f32[4,256,256]{2,1,0:T(8,128)} %refl.1, f32[4,128,256]{2,1,0:T(8,128)} %tfac.1, f32[1024,256]{1,0:T(8,128)} %eig.1), custom_call_target="tpu_custom_call" | custom-call | tf_op jit(solution)/shard_map/sweep/pallas_call | solution.py:927
  81.4 1.0 %copy.6 = f32[1024,256]{1,0:T(8,128)} copy(f32[1024,256]{1,0:T(8,128)S(1)} %sweep.1) | data formatting | bytes 2097152

commit v9 on v8

--- a/solution.py
+++ b/solution.py
@@ -255,14 +255,14 @@
     def greet(target):
         pl.semaphore_signal(barrier, inc=1, device_id=target, device_id_type=MESH)
 
+    @pl.when(has_beyond)
+    def _():
+        greet((beyond, partner))
+        greet((beyond, col))
+
     greet((row, partner))
     greet((mate, partner))
     greet((mate, col))
-
-    @pl.when(has_beyond)
-    def _():
-        greet((beyond, col))
-        greet((beyond, partner))
 
     @pl.when(inner)
     def _():

time: 82.6 us -> 82.6 us (level)
  no operation moved by 1% of the time
where the time goes in v9:
time: 82.6 us; the launch traced here: 82.4 us
  Pallas kernels  81.4 us (99%)
  local copies, waits for them, and re-layouts  0.97 us (1%)
    pallas_call x1, Pallas kernels, on_device(): pl.pallas_call(functools.partial(line_kernel, rows_n), out_shape=pltpu.VM...  81.4 us

profile of v9, /device:TPU:3, one launch (start us, length us, event | category | flops | bytes accessed | tf_op | source)
XLA Modules:
  0.0 82.4 jit_solution(5179789793403698496)
XLA Ops:
  0.0 81.4 %sweep.1 = f32[1024,256]{1,0:T(8,128)S(1)} custom-call(s32[2,4]{1,0:T(2,128)} %sched_all.1, f32[4,256,256]{2,1,0:T(8,128)} %refl.1, f32[4,128,256]{2,1,0:T(8,128)} %tfac.1, f32[1024,256]{1,0:T(8,128)} %eig.1), custom_call_target="tpu_custom_call" | custom-call | tf_op jit(solution)/shard_map/sweep/pallas_call | solution.py:927
  81.4 1.0 %copy.6 = f32[1024,256]{1,0:T(8,128)} copy(f32[1024,256]{1,0:T(8,128)S(1)} %sweep.1) | data formatting | bytes 2097152
